TPU v7x, 32 devices: a whole 2x2x4 slice. The times are simulated.
32 devices in a mesh: row: 4 (over x, core), col: 8 (over z, y).
Axes of the slice: x: 2, y: 2, z: 4, core: 2. Of those that a mesh axis runs over, the one named last changes fastest.
Arguments:
- features: bfloat16 [4096, 256], P(('row', 'col')), may hold values from -192 to 192
- grad_out: bfloat16 [4096, 256], P(('row', 'col')), may hold values from -192 to 192
- tile_weight: bfloat16 [2048, 128, 128], P(('row', 'col')), may hold values from 0 to 256, as said below
- tile_list: int32 [128, 3, 32], P(('row', 'col')), may hold values from -1 to 63, as said below
Outputs:
- aggregated: bfloat16 [4096, 256], P(('row', 'col'))
- feature_grad: bfloat16 [4096, 256], P(('row', 'col'))
Inputs may be any that keep to these rules, and one draw needn't show every extreme that they name: `tile_list`: each column of a list is a slot (tile number, source block below 1, destination block below 8); tile number -1 marks an empty slot, whose blocks are 0. The tile numbers listed by one device are distinct and are 0 to n - 1 for some n between 40 and 64; some device lists all 64. On every device some step has all 32 slots used. Stored tiles that no slot lists take no part. `tile_weight`: entries are whole numbers.
All inputs are finite; a program needn't handle non-finite values.
Results may differ from a plain program's by a relative error of at most 0.017.
Values may be sent and summed in bfloat16 or wider, within the bound.
No kernel may reach another device: no remote copies, remote signals or barrier semaphores. Data moves between devices by JAX's collectives and lax.ppermute only.
A program may use at most 64 MiB of HBM per device.

v0:
```python
import math

import jax
import jax.numpy as jnp
from jax import lax
from jax.sharding import PartitionSpec as P


def passed_along(value, axis, steps):
    count = lax.axis_size(axis)
    pairs = [(source, (source + steps) % count) for source in range(count)]
    return lax.ppermute(value, axis, pairs)


def local(features, grad_out, tile_weight, tile_list):
    step_count = lax.axis_size("row")
    columns = lax.axis_size("col")
    row_pos = lax.axis_index("row")
    slot_count = tile_list.shape[2]
    tiles_here = tile_weight.shape[0]
    tile_len = tile_weight.shape[1]
    feat_width = features.shape[1]
    src_blocks = features.shape[0] // tile_len
    dst_blocks = columns * (grad_out.shape[0] // tile_len)
    flat_ids = tile_list[:, 0, :].reshape(-1)
    flat_step = jnp.arange(step_count * slot_count, dtype=jnp.int32) // slot_count
    matches = (flat_ids[None, :] == jnp.arange(tiles_here, dtype=jnp.int32)[:, None]).astype(
        jnp.int32
    )
    tile_used = jnp.sum(matches, axis=1)
    tile_step = jnp.sum(matches * flat_step[None, :], axis=1)
    tile_src = jnp.sum(matches * tile_list[:, 1, :].reshape(-1)[None, :], axis=1)
    tile_dst = jnp.sum(matches * tile_list[:, 2, :].reshape(-1)[None, :], axis=1)
    owner_row = (row_pos - tile_step) % step_count
    src_slot = owner_row * src_blocks + tile_src
    used_float = tile_used.astype(jnp.float32)
    row_sums = jnp.sum(tile_weight, axis=2, dtype=jnp.float32)
    col_sums = jnp.sum(tile_weight, axis=1, dtype=jnp.float32)
    dst_pick = (tile_dst[:, None] == jnp.arange(dst_blocks, dtype=jnp.int32)[None, :]).astype(
        jnp.float32
    ) * used_float[:, None]
    src_pick = (
        src_slot[:, None] == jnp.arange(step_count * src_blocks, dtype=jnp.int32)[None, :]
    ).astype(jnp.float32) * used_float[:, None]
    dst_terms = jnp.dot(dst_pick.T, row_sums, precision=lax.Precision.HIGHEST).reshape(-1)
    src_terms = jnp.dot(src_pick.T, col_sums, precision=lax.Precision.HIGHEST).reshape(-1)
    src_scale = lax.rsqrt(1.0 + lax.psum_scatter(src_terms, "row", scatter_dimension=0, tiled=True))
    dst_scale = lax.rsqrt(1.0 + lax.psum_scatter(dst_terms, "col", scatter_dimension=0, tiled=True))
    scaled = (features.astype(jnp.float32) * src_scale[:, None]).astype(jnp.bfloat16)
    scaled = scaled.reshape(src_blocks, tile_len, feat_width)
    scaled_grads = (grad_out.astype(jnp.float32) * dst_scale[:, None]).astype(jnp.bfloat16)
    grad_rows = lax.all_gather(scaled_grads, "col", axis=0, tiled=True).reshape(
        dst_blocks, tile_len, feat_width
    )

    def pick_tiles(list_step):
        tile_ids = tile_list[list_step, 0]
        keep_mask = (tile_ids >= 0).astype(jnp.bfloat16)
        chosen = tile_weight[jnp.maximum(tile_ids, 0)] * keep_mask[:, None, None]
        return (chosen, tile_list[list_step, 1], tile_list[list_step, 2])

    def backward_add(accum_total, rows, list_step):
        chosen, src_index, dst_index = pick_tiles(list_step)
        products = jnp.einsum(
            "kij,kif->kjf", chosen, rows[dst_index], preferred_element_type=jnp.float32
        )
        return accum_total.at[src_index].add(products)

    def grad_step(grad_state, step_pos):
        return backward_add(grad_state, grad_rows, step_count - 1 - step_pos)

    def grad_move(grad_state):
        return passed_along(grad_state.astype(jnp.bfloat16), "row", -1).astype(grad_state.dtype)

    partial_zero = jnp.zeros((dst_blocks, tile_len, feat_width), jnp.float32)
    everything = lax.all_gather(scaled, "row", axis=0, tiled=True)
    batch_size = math.gcd(tiles_here, 16)

    def tile_batch(loop_index, partial_value):
        first_tile = loop_index * batch_size
        tile_block = lax.dynamic_slice_in_dim(tile_weight, first_tile, batch_size, 0)
        keep_mask = lax.dynamic_slice_in_dim(tile_used, first_tile, batch_size, 0).astype(
            jnp.bfloat16
        )
        src_index = lax.dynamic_slice_in_dim(src_slot, first_tile, batch_size, 0)
        dst_index = lax.dynamic_slice_in_dim(tile_dst, first_tile, batch_size, 0)
        chosen = tile_block * keep_mask[:, None, None]
        products = jnp.einsum(
            "kij,kjf->kif", chosen, everything[src_index], preferred_element_type=jnp.float32
        )
        return partial_value.at[dst_index].add(products)

    partial_value = lax.fori_loop(0, tiles_here // batch_size, tile_batch, partial_zero)

    def grad_loop(step_pos, grad_state):
        return grad_move(grad_step(grad_state, step_pos))

    grad_state = lax.fori_loop(
        0, step_count - 1, grad_loop, jnp.zeros((src_blocks, tile_len, feat_width), jnp.float32)
    )
    grad_state = grad_step(grad_state, step_count - 1)
    summed = lax.psum_scatter(
        partial_value.reshape(dst_blocks * tile_len, feat_width).astype(jnp.bfloat16),
        "col",
        scatter_dimension=0,
        tiled=True,
    ).astype(jnp.float32)
    aggregated = (summed * dst_scale[:, None]).astype(jnp.bfloat16)
    grads = grad_state.reshape(src_blocks * tile_len, feat_width)
    feature_grad = (grads * src_scale[:, None]).astype(jnp.bfloat16)
    return (aggregated, feature_grad)


def solution(mesh):
    return jax.shard_map(
        local,
        mesh=mesh,
        in_specs=(
            P(("row", "col"), None),
            P(("row", "col"), None),
            P(("row", "col"), None, None),
            P(("row", "col"), None, None),
        ),
        out_specs=(P(("row", "col"), None), P(("row", "col"), None)),
        check_vma=False,
    )
```

profile of v0, /device:TPU:0, one launch (start us, length us, event | category | flops | bytes accessed | tf_op | source)
XLA Modules:
  0.0 244.0 jit_solution(11328118093270040016)
XLA Ops:
  7.2 0.8 fusion.26
  8.1 0.7 fusion.27
  8.8 0.7 fusion.29
  9.4 0.7 maximum_bitcast_fusion.1
  10.1 0.7 fusion.34
  10.8 0.7 copy.13
  11.5 1.3 dynamic-slice.2
  12.9 1.2 dynamic-slice
  15.4 0.1 mul.136
  15.4 0.1 mul.141
  15.5 0.1 eq.22
  15.6 0.2 select_reduce_fusion.1
  15.8 2.3 convert_reduce_fusion
  18.0 0.3 convolution_bitcast_fusion.1
  18.3 8.4 %all-reduce = f32[512]{0:T(512)S(1)} all-reduce(f32[512]{0:T(512)S(1)} %convolution_bitcast_fusion.1), channel_id=3, replica_groups=mesh['row'=4,'col'=8] {'row'}, use_global_device_ids=true, to_apply=%region_5.6.clone | all-reduce | flops 512 | bytes 4096
  26.7 0.3 convolution_bitcast_fusion
  26.9 21.7 %all-reduce.1 = f32[1024]{0:T(1024)S(1)} all-reduce(f32[1024]{0:T(1024)S(1)} %convolution_bitcast_fusion), channel_id=5, replica_groups=mesh['row'=4,'col'=8] {'col'}, use_global_device_ids=true, to_apply=%region_11.12.clone | all-reduce | flops 1024 | bytes 8192
  48.6 0.1 fusion.30
  48.7 0.1 multiply_convert_fusion
  48.8 31.5 %all_gather.7 = bf16[1024,256]{1,0:T(8,128)(2,1)S(1)} all-gather(bf16[128,256]{1,0:T(8,128)(2,1)S(1)} %multiply_convert_fusion), channel_id=1, replica_groups=mesh['row'=4,'col'=8] {'col'}, dimensions={0}, use_global_device_ids=true | all-gather | bytes 589824 | tf_op jit(solution)/shard_map/all_gather | solution.py:52
  80.3 1.7 gather_fusion.3
  82.1 2.0 gather_fusion.4
  84.1 5.0 %fusion.13 = f32[32,128,256]{2,1,0:T(8,128)} fusion(bf16[32,128,256]{2,1,0:T(8,128)(2,1)} %gather_fusion.4, bf16[32,128,128]{2,1,0:T(8,128)(2,1)} %gather_fusion.3, bf16[32]{0:T(256)(128)(2,1)S(1)} %fusion.26), kind=kOutput, calls=%fused_computation.41 | convolution fusion | flops 268959744 | bytes 7340096 | tf_op jit(solution)/shard_map/kij,kif->kjf/dot_general | solution.py:64
  89.0 49.5 %while.30 = (s32[]{:T(128)}, f32[1,128,256]{2,1,0:T(8,128)S(1)}, s32[4,3,32]{2,1,0:T(4,128)S(1)}, bf16[64,128,128]{2,1,0:T(8,128)(2,1)S(1)}, bf16[8,128,256]{2,1...) while((s32[]{:T(128)}, f32[1,128,256]{2,1,0:T(8,128)S(1)}, ...), condition=%wide.region_14.15_spmd.clone, body=%wide.region_12.14_spmd.clone.sunk | while | flops 270109056 | bytes 35530608 | solution.py:98
  89.1 1.7 gather_fusion.2
  90.9 0.7 gather_fusion.1
  91.6 4.3 %fusion.57 = f32[32,128,256]{2,1,0:T(8,128)} fusion(bf16[32,128,256]{2,1,0:T(8,128)(2,1)S(1)} %gather_fusion.1, bf16[32,128,128]{2,1,0:T(8,128)(2,1)} %gather_fusion.2, bf16[32]{0:T(256)(128)(2,1)S(1)} %fusion.56), kind=kOutput, calls=%fused_computation.17.clone.1 | convolution fusion | flops 268959744 | bytes 7340096 | tf_op jit(solution)/shard_map/while/body/eval_jaxpr/kij,kif->kjf/dot_general | solution.py:64
  95.9 6.4 %scatter_fusion.1 = f32[128,256,1]{1,0,2:T(8,128)S(1)} fusion(f32[128,256,1]{1,0,2:T(8,128)S(1)} %select_bitcast_fusion.2, s32[32]{0:T(128)S(1)} %fusion.54, f32[32,128,256]{2,1,0:T(8,128)} %fusion.57), kind=kCustom, calls=%fused_computation.6.clone.clone.1 | custom fusion | flops 1048576 | bytes 12583040 | tf_op jit(solution)/shard_map/while/body/eval_jaxpr/scatter-add | solution.py:67
  102.4 1.9 collective-permute-done
  104.5 1.7 gather_fusion.2
  106.2 0.7 gather_fusion.1
  106.9 4.3 %fusion.57 = f32[32,128,256]{2,1,0:T(8,128)} fusion(bf16[32,128,256]{2,1,0:T(8,128)(2,1)S(1)} %gather_fusion.1, bf16[32,128,128]{2,1,0:T(8,128)(2,1)} %gather_fusion.2, bf16[32]{0:T(256)(128)(2,1)S(1)} %fusion.56), kind=kOutput, calls=%fused_computation.17.clone.1 | convolution fusion | flops 268959744 | bytes 7340096 | tf_op jit(solution)/shard_map/while/body/eval_jaxpr/kij,kif->kjf/dot_general | solution.py:64
  111.2 6.4 %scatter_fusion.1 = f32[128,256,1]{1,0,2:T(8,128)S(1)} fusion(f32[128,256,1]{1,0,2:T(8,128)S(1)} %select_bitcast_fusion.2, s32[32]{0:T(128)S(1)} %fusion.54, f32[32,128,256]{2,1,0:T(8,128)} %fusion.57), kind=kCustom, calls=%fused_computation.6.clone.clone.1 | custom fusion | flops 1048576 | bytes 12583040 | tf_op jit(solution)/shard_map/while/body/eval_jaxpr/scatter-add | solution.py:67
  117.7 1.8 collective-permute-start
  119.5 1.9 collective-permute-done
  121.6 1.7 gather_fusion.2
  123.3 0.7 gather_fusion.1
  124.0 4.3 %fusion.57 = f32[32,128,256]{2,1,0:T(8,128)} fusion(bf16[32,128,256]{2,1,0:T(8,128)(2,1)S(1)} %gather_fusion.1, bf16[32,128,128]{2,1,0:T(8,128)(2,1)} %gather_fusion.2, bf16[32]{0:T(256)(128)(2,1)S(1)} %fusion.56), kind=kOutput, calls=%fused_computation.17.clone.1 | convolution fusion | flops 268959744 | bytes 7340096 | tf_op jit(solution)/shard_map/while/body/eval_jaxpr/kij,kif->kjf/dot_general | solution.py:64
  128.3 6.4 %scatter_fusion.1 = f32[128,256,1]{1,0,2:T(8,128)S(1)} fusion(f32[128,256,1]{1,0,2:T(8,128)S(1)} %select_bitcast_fusion.2, s32[32]{0:T(128)S(1)} %fusion.54, f32[32,128,256]{2,1,0:T(8,128)} %fusion.57), kind=kCustom, calls=%fused_computation.6.clone.clone.1 | custom fusion | flops 1048576 | bytes 12583040 | tf_op jit(solution)/shard_map/while/body/eval_jaxpr/scatter-add | solution.py:67
  134.8 1.8 collective-permute-start
  136.6 1.9 collective-permute-done
  138.6 6.3 %scatter_fusion.2 = f32[128,256,1]{1,0,2:T(8,128)S(1)} fusion(f32[128,256,1]{1,0,2:T(8,128)S(1)} %bitcast.83, s32[32]{0:T(128)S(1)} %fusion.27, f32[32,128,256]{2,1,0:T(8,128)} %fusion.13), kind=kCustom, calls=%fused_computation.7 | custom fusion | flops 1048576 | bytes 12583040 | tf_op jit(solution)/shard_map/scatter-add | solution.py:67
  144.9 0.7 fusion.16
  145.6 6.0 %all-gather = bf16[512,256]{1,0:T(8,128)(2,1)S(1)} all-gather(bf16[128,256]{1,0:T(8,128)(2,1)S(1)} %get-tuple-element.329), channel_id=2, replica_groups=mesh['row'=4,'col'=8] {'row'}, dimensions={0}, use_global_device_ids=true | all-gather | bytes 327680 | tf_op jit(solution)/shard_map/all_gather | solution.py:76
  151.6 0.1 broadcast_in_dim.51
  151.7 23.5 %while.29 = (s32[]{:T(128)}, f32[8,128,256]{2,1,0:T(8,128)S(1)}, s32[64]{0:T(128)S(1)}, bf16[64,128,128]{2,1,0:T(8,128)(2,1)}, s32[64]{0:T(128)S(1)}, /*index=5*...) while((s32[]{:T(128)}, f32[8,128,256]{2,1,0:T(8,128)S(1)}, ...), condition=%wide.region_8.9_spmd, body=%wide.region_6.8_spmd.sunk | while | flops 135005296 | bytes 12063463 | solution.py:93
  151.7 0.1 dynamic-slice_convert_fusion.2
  151.9 1.6 gather_fusion
  153.5 1.9 fusion.51
  155.4 2.2 scatter_fusion
  157.6 0.1 dynamic-slice_convert_fusion.2
  157.7 1.6 gather_fusion
  159.3 1.9 fusion.51
  161.2 2.2 scatter_fusion
  163.4 0.1 dynamic-slice_convert_fusion.2
  163.6 1.6 gather_fusion
  165.2 1.9 fusion.51
  167.1 2.2 scatter_fusion
  169.5 1.6 gather_fusion
  171.1 1.9 fusion.51
  173.0 2.2 scatter_fusion
  175.2 0.8 convert_element_type.102
  176.0 59.6 %reduce-scatter.2.cloned.1.call-done = bf16[128,256]{1,0:T(8,128)(2,1)} async-done(((bf16[1024,256]{1,0:T(8,128)(2,1)}), bf16[128,256]{1,0:T(8,128)(2,1)}) %reduce-scatter.2.cloned.1.call-update) | async-done | bytes 65552 | tf_op jit(solution)/shard_map/reduce_scatter | solution.py:102
  235.7 1.6 multiply_convert_fusion.1
  (58 shorter events, 0.9 us)
Async XLA Ops:
  7.2 73.1 %copy-start = (bf16[64,128,128]{2,1,0:T(8,128)(2,1)S(1)}, bf16[64,128,128]{2,1,0:T(8,128)(2,1)}, u32[]{:S(2)}) copy-start(bf16[64,128,128]{2,1,0:T(8,128)(2,1)} %param.10) | copy-start | bytes 6291460
  7.2 41.5 %copy-start.3 = (bf16[128,256]{1,0:T(8,128)(2,1)S(1)}, bf16[128,256]{1,0:T(8,128)(2,1)}, u32[]{:S(2)}) copy-start(bf16[128,256]{1,0:T(8,128)(2,1)} %param.9) | copy-start | bytes 196612
  7.2 228.5 %reduce-scatter.2.cloned.1.call-start = ((), (), s32[]{:S(2)}) async-start(), calls=%async_computation.1 | async-start | bytes 589824 | tf_op jit(solution)/shard_map/reduce_scatter | solution.py:102
  95.9 8.4 %copy-start.1 = (bf16[64,128,128]{2,1,0:T(8,128)(2,1)S(1)}, bf16[64,128,128]{2,1,0:T(8,128)(2,1)}, u32[]{:S(2)}) copy-start(bf16[64,128,128]{2,1,0:T(8,128)(2,1)} %get-tuple-element.478) | copy-start | bytes 6291460 | tf_op jit(solution)/shard_map/while
  102.3 2.0 collective-permute-start
  111.2 10.2 %copy-start.1 = (bf16[64,128,128]{2,1,0:T(8,128)(2,1)S(1)}, bf16[64,128,128]{2,1,0:T(8,128)(2,1)}, u32[]{:S(2)}) copy-start(bf16[64,128,128]{2,1,0:T(8,128)(2,1)} %get-tuple-element.478) | copy-start | bytes 6291460 | tf_op jit(solution)/shard_map/while
  117.7 3.7 %collective-permute-start = (bf16[1,128,256]{2,1,0:T(8,128)(2,1)S(1)}, bf16[1,128,256]{2,1,0:T(8,128)(2,1)S(1)}, u32[]{:S(2)}, u32[]{:S(2)}) collective-permute-start(bf16[1,128,256]{2,1,0:T(8,128)(2,1)S(1)} %convert_bitcast_fusion.2), channel_id=1, source_target_pairs={{0,24},{8,0},{16,8},{24,16},{1,25},{9,1},{17,9},{25,17},{2,26},{10... | collective-permute-start | bytes 196616 | tf_op jit(solution)/shard_map/while/body/eval_jaxpr/ppermute | solution.py:12
  128.3 10.2 %copy-start.1 = (bf16[64,128,128]{2,1,0:T(8,128)(2,1)S(1)}, bf16[64,128,128]{2,1,0:T(8,128)(2,1)}, u32[]{:S(2)}) copy-start(bf16[64,128,128]{2,1,0:T(8,128)(2,1)} %get-tuple-element.478) | copy-start | bytes 6291460 | tf_op jit(solution)/shard_map/while
  134.8 3.7 %collective-permute-start = (bf16[1,128,256]{2,1,0:T(8,128)(2,1)S(1)}, bf16[1,128,256]{2,1,0:T(8,128)(2,1)S(1)}, u32[]{:S(2)}, u32[]{:S(2)}) collective-permute-start(bf16[1,128,256]{2,1,0:T(8,128)(2,1)S(1)} %convert_bitcast_fusion.2), channel_id=1, source_target_pairs={{0,24},{8,0},{16,8},{24,16},{1,25},{9,1},{17,9},{25,17},{2,26},{10... | collective-permute-start | bytes 196616 | tf_op jit(solution)/shard_map/while/body/eval_jaxpr/ppermute | solution.py:12
  138.6 6.4 %copy-start.2 = (bf16[128,256]{1,0:T(8,128)(2,1)S(1)}, bf16[128,256]{1,0:T(8,128)(2,1)}, u32[]{:S(2)}) copy-start(bf16[128,256]{1,0:T(8,128)(2,1)} %param.8) | copy-start | bytes 196612
Sparse Core Ops, SparseCore 0:
  176.2 59.4 reduce-scatter.1
where the time goes:
time: 245 us; the launch traced here: 244 us
  blocking collectives  67.5 us (28%)
  waiting for transfers between devices  65.3 us (27%)
  other arithmetic  43.9 us (18%)
  matrix products  25.9 us (11%)
  local copies, waits for them, and re-layouts  21.7 us (9%)
  between operations  15.4 us (6%)
  starting transfers between devices  3.77 us (2%)
    reduce_scatter x1, waiting for transfers between devices, local(): lax.psum_scatter(partial_value.reshape(dst_blocks * tile_len, feat_width)...  59.6 us
    all_gather x1, blocking collectives, local(): lax.all_gather(scaled_grads, 'col', axis=0, tiled=True)  31.5 us
    unnamed x2, blocking collectives  30 us
    scatter-add x4, other arithmetic, backward_add(): return accum_total.at[src_index].add(products)  25.6 us
    dot_general x4, matrix products, backward_add(): jnp.einsum('kij,kif->kjf', chosen, rows[dst_index], preferred_element_typ...  17.9 us
    scatter-add x4, other arithmetic, tile_batch(): return partial_value.at[dst_index].add(products)  8.78 us
    dot_general x4, matrix products, tile_batch(): jnp.einsum('kij,kjf->kif', chosen, everything[src_index], preferred_eleme...  7.47 us
    gather x4, local copies, waits for them, and re-layouts, pick_tiles(): chosen = tile_weight[jnp.maximum(tile_ids, 0)] * keep_mask[:, None, None]  6.93 us
  transfers between devices with their start and end apart: 4, of which 4 were waited for; matrix products, arithmetic and copies ran while one was open for 0% of the time, Pallas kernels for 0%

commit v1 on v0

v1 whole, which is shorter than its diff:
```python
import functools

import jax
import jax.numpy as jnp
from jax import lax
from jax.experimental import pallas as pl
from jax.experimental.pallas import tpu as pltpu
from jax.sharding import PartitionSpec as P

F32 = jnp.float32
BF16 = jnp.bfloat16
PARTS = 3


def round_up(value, step):
    return -(-value // step) * step


def message_rows(count, width):
    part_rows = count // width
    return part_rows, round_up(PARTS * part_rows, 16)


def pack_counts(counts, width):
    rows, total = counts.shape
    part_rows = total // width
    row = lax.broadcasted_iota(jnp.int32, (rows, width), 0)
    value = jnp.zeros((rows, width), F32)
    for i in range(part_rows):
        here = row == i
        for part in range(1, PARTS):
            here = here | (row == part * part_rows + i)
        value = jnp.where(here, counts[:, i * width : (i + 1) * width], value)
    high = value.astype(BF16).astype(F32)
    middle = (value - high).astype(BF16).astype(F32)
    low = value - high - middle
    packed = jnp.where(row < part_rows, high, jnp.where(row < 2 * part_rows, middle, low))
    return packed.astype(BF16)


def unpack_scales(parts, part_rows):
    total = parts[0:part_rows]
    for part in range(1, PARTS):
        total = total + parts[part * part_rows : (part + 1) * part_rows]
    return lax.rsqrt(1.0 + total)


def scale_column(scales, block, tile_len):
    width = scales.shape[1]
    row, first = divmod(block * tile_len, width)
    line = scales[row : row + 1, first : first + tile_len]
    return jnp.broadcast_to(line, (tile_len, tile_len)).T


def scaled_rows(rows, column):
    width = rows.shape[1]
    tile_len = column.shape[1]
    pieces = [
        rows[:, i * tile_len : (i + 1) * tile_len].astype(F32) * column
        for i in range(width // tile_len)
    ]
    return jnp.concatenate(pieces, axis=1)


def place_kernel(
    chunks,
    src_blocks,
    list_ref,
    features_ref,
    grads_ref,
    tiles_hbm,
    adjacency_ref,
    src_send_ref,
    dst_send_ref,
    tiles_ref,
    total_ref,
    line_ref,
    where_ref,
    sems,
):
    tile_count, tile_len, _ = tiles_ref.shape
    step_count, _, slot_count = list_ref.shape
    width = features_ref.shape[1]
    dst_blocks = adjacency_ref.shape[0] // tile_len
    slots = adjacency_ref.shape[1] // tile_len
    pairs = dst_blocks * slots
    per_chunk = tile_count // chunks

    def chunk_copy(i):
        window = pl.ds(i * per_chunk, per_chunk)
        return pltpu.make_async_copy(tiles_hbm.at[window], tiles_ref.at[window], sems.at[i])

    for i in range(chunks):
        chunk_copy(i).start()

    @pl.loop(0, tile_count)
    def _(t):
        where_ref[t] = pairs

    row_pos = lax.axis_index("row")
    for step in range(step_count):
        owner = lax.rem(row_pos - step + step_count, step_count)

        @pl.loop(0, slot_count)
        def _(k):
            t = list_ref[step, 0, k]
            pair = list_ref[step, 2, k] * slots + owner * src_blocks + list_ref[step, 1, k]
            where_ref[jnp.where(t >= 0, t, tile_count)] = pair

    @pl.loop(0, pairs)
    def _(p):
        total_ref[p] = jnp.zeros((tile_len, tile_len), F32)

    total_ref[pairs] = jnp.zeros((tile_len, tile_len), F32)
    for i in range(chunks):
        chunk_copy(i).wait()

        @pl.loop(i * per_chunk, (i + 1) * per_chunk)
        def _(t):
            p = where_ref[t]
            total_ref[p] = total_ref[p] + tiles_ref[t].astype(F32)

    src_rows = src_send_ref.shape[1] - features_ref.shape[0]
    dst_rows = dst_send_ref.shape[1] - grads_ref.shape[0]
    col_sums = tuple(jnp.zeros((8, tile_len), F32) for _ in range(slots))

    def block_row(e, sums):
        first = pl.multiple_of(e * tile_len, tile_len)
        across = jnp.zeros((tile_len, tile_len), F32)
        out = []
        for s in range(slots):
            block = total_ref[e * slots + s]
            adjacency_ref[pl.ds(first, tile_len), s * tile_len : (s + 1) * tile_len] = block.astype(
                BF16
            )
            across = across + block
            out.append(sums[s] + jnp.sum(block.reshape(tile_len // 8, 8, tile_len), axis=0))
        high = across.astype(BF16)
        low = (across - high.astype(F32)).astype(BF16)
        ones = jnp.ones((dst_rows, tile_len), BF16)
        contract = (((1,), (1,)), ((), ()))
        line_ref[:, pl.ds(first, tile_len)] = lax.dot_general(
            ones, high, contract, preferred_element_type=F32
        ) + lax.dot_general(ones, low, contract, preferred_element_type=F32)
        return tuple(out)

    if dst_blocks <= 8:
        for e in range(dst_blocks):
            col_sums = block_row(e, col_sums)
    else:
        col_sums = lax.fori_loop(0, dst_blocks, block_row, col_sums)
    src_line = jnp.concatenate(
        [
            jnp.broadcast_to(jnp.sum(sums, axis=0, keepdims=True), (src_rows, tile_len))
            for sums in col_sums
        ],
        axis=1,
    )
    src_packed = pack_counts(src_line, width)
    dst_packed = pack_counts(line_ref[...], width)
    for j in range(src_send_ref.shape[0]):
        src_send_ref[j, : features_ref.shape[0]] = features_ref[...]
        src_send_ref[j, features_ref.shape[0] :] = src_packed
    for j in range(dst_send_ref.shape[0]):
        dst_send_ref[j, : grads_ref.shape[0]] = grads_ref[...]
        dst_send_ref[j, grads_ref.shape[0] :] = dst_packed


def forward_kernel(
    src_blocks, message_ref, adjacency_ref, partial_ref, own_scale_ref, scaled_ref
):
    senders, rows, width = message_ref.shape
    dst_blocks, tile_len, _ = partial_ref.shape
    body = src_blocks * tile_len
    part_rows = senders * body // width
    parts = message_ref[0, body:].astype(F32)
    for j in range(1, senders):
        parts = parts + message_ref[j, body:].astype(F32)
    scales = unpack_scales(parts, part_rows)
    row_pos = lax.axis_index("row")
    for j in range(senders):
        for b in range(src_blocks):
            column = scale_column(scales, j * src_blocks + b, tile_len)
            first = (j * src_blocks + b) * tile_len
            rows_here = message_ref[j, b * tile_len : (b + 1) * tile_len]
            scaled_ref[first : first + tile_len] = scaled_rows(rows_here, column).astype(BF16)

            @pl.when(row_pos == j)
            def _():
                own_scale_ref[b * tile_len : (b + 1) * tile_len] = column

    def one(e):
        first = pl.multiple_of(e * tile_len, tile_len)
        partial_ref[e] = jnp.dot(
            adjacency_ref[pl.ds(first, tile_len)], scaled_ref[...], preferred_element_type=F32
        ).astype(BF16)

    if dst_blocks <= 8:
        for e in range(dst_blocks):
            one(e)
    else:
        pl.loop(0, dst_blocks)(one)


def backward_kernel(
    own_blocks, message_ref, adjacency_ref, partial_ref, own_scale_ref, scaled_ref
):
    senders, rows, width = message_ref.shape
    slots, tile_len, _ = partial_ref.shape
    body = own_blocks * tile_len
    part_rows = senders * body // width
    parts = message_ref[0, body:].astype(F32)
    for j in range(1, senders):
        parts = parts + message_ref[j, body:].astype(F32)
    scales = unpack_scales(parts, part_rows)
    col_pos = lax.axis_index("col")
    for j in range(senders):
        for b in range(own_blocks):
            column = scale_column(scales, j * own_blocks + b, tile_len)
            first = (j * own_blocks + b) * tile_len
            rows_here = message_ref[j, b * tile_len : (b + 1) * tile_len]
            scaled_ref[first : first + tile_len] = scaled_rows(rows_here, column).astype(BF16)

            @pl.when(col_pos == j)
            def _():
                own_scale_ref[b * tile_len : (b + 1) * tile_len] = column

    for s in range(slots):
        partial_ref[s] = lax.dot_general(
            adjacency_ref[:, s * tile_len : (s + 1) * tile_len],
            scaled_ref[...],
            (((0,), (0,)), ((), ())),
            preferred_element_type=F32,
        ).astype(BF16)


def finish_kernel(received_ref, scale_ref, out_ref):
    senders, rows, width = received_ref.shape
    tile_len = scale_ref.shape[1]
    total = received_ref[0].astype(F32)
    for j in range(1, senders):
        total = total + received_ref[j].astype(F32)
    column = scale_ref[...]
    for i in range(width // tile_len):
        lanes = slice(i * tile_len, (i + 1) * tile_len)
        out_ref[:, lanes] = (total[:, lanes] * column).astype(BF16)


VMEM = pl.BlockSpec(memory_space=pltpu.VMEM)


def local(features, grad_out, tile_weight, tile_list):
    row_count = lax.axis_size("row")
    col_count = lax.axis_size("col")
    tile_count, tile_len, _ = tile_weight.shape
    width = features.shape[1]
    src_blocks = features.shape[0] // tile_len
    own_blocks = grad_out.shape[0] // tile_len
    slots = row_count * src_blocks
    dst_blocks = col_count * own_blocks
    _, src_rows = message_rows(slots * tile_len, width)
    _, dst_rows = message_rows(dst_blocks * tile_len, width)
    chunks = 4 if tile_count % 4 == 0 else 1
    shape = jax.ShapeDtypeStruct

    adjacency, src_send, dst_send = pl.pallas_call(
        functools.partial(place_kernel, chunks, src_blocks),
        out_shape=(
            shape((dst_blocks * tile_len, slots * tile_len), BF16),
            shape((row_count, features.shape[0] + src_rows, width), BF16),
            shape((col_count, grad_out.shape[0] + dst_rows, width), BF16),
        ),
        in_specs=[
            pl.BlockSpec(memory_space=pltpu.SMEM),
            VMEM,
            VMEM,
            pl.BlockSpec(memory_space=pl.ANY),
        ],
        out_specs=(VMEM, VMEM, VMEM),
        scratch_shapes=[
            pltpu.VMEM((tile_count, tile_len, tile_len), BF16),
            pltpu.VMEM((dst_blocks * slots + 1, tile_len, tile_len), F32),
            pltpu.VMEM((dst_rows, dst_blocks * tile_len), F32),
            pltpu.SMEM((tile_count + 1,), jnp.int32),
            pltpu.SemaphoreType.DMA((chunks,)),
        ],
        name="place",
    )(tile_list, features, grad_out, tile_weight)

    src_message = lax.all_to_all(src_send, "row", 0, 0, tiled=True)
    dst_message = lax.all_to_all(dst_send, "col", 0, 0, tiled=True)
    partial, src_scale = pl.pallas_call(
        functools.partial(forward_kernel, src_blocks),
        out_shape=(
            shape((dst_blocks, tile_len, width), BF16),
            shape((features.shape[0], tile_len), F32),
        ),
        in_specs=[VMEM, VMEM],
        out_specs=(VMEM, VMEM),
        scratch_shapes=[pltpu.VMEM((slots * tile_len, width), BF16)],
        name="forward",
    )(src_message, adjacency)
    dst_partials = lax.all_to_all(partial, "col", 0, 0, tiled=True)
    back_partial, dst_scale = pl.pallas_call(
        functools.partial(backward_kernel, own_blocks),
        out_shape=(
            shape((slots, tile_len, width), BF16),
            shape((grad_out.shape[0], tile_len), F32),
        ),
        in_specs=[VMEM, VMEM],
        out_specs=(VMEM, VMEM),
        scratch_shapes=[pltpu.VMEM((dst_blocks * tile_len, width), BF16)],
        name="backward",
    )(dst_message, adjacency)
    src_partials = lax.all_to_all(back_partial, "row", 0, 0, tiled=True)

    def finish(received, scale, count, rows):
        return pl.pallas_call(
            finish_kernel,
            out_shape=shape((rows, width), BF16),
            in_specs=[VMEM, VMEM],
            out_specs=VMEM,
            name="finish",
        )(received.reshape(count, rows, width), scale)

    feature_grad = finish(src_partials, src_scale, row_count, features.shape[0])
    aggregated = finish(dst_partials, dst_scale, col_count, grad_out.shape[0])
    return (aggregated, feature_grad)


def solution(mesh):
    return jax.shard_map(
        local,
        mesh=mesh,
        in_specs=(
            P(("row", "col"), None),
            P(("row", "col"), None),
            P(("row", "col"), None, None),
            P(("row", "col"), None, None),
        ),
        out_specs=(P(("row", "col"), None), P(("row", "col"), None)),
        check_vma=False,
    )
```

time: 245 us -> 71.3 us (0.29)
  blocking collectives: 67.5 us -> 11.2 us
  other arithmetic: 43.9 us -> 0 us
  waiting for transfers between devices: 65.3 us -> 28.4 us
  matrix products: 25.9 us -> 0 us
  local copies, waits for them, and re-layouts: 21.7 us -> 2.01 us
  between operations: 15.4 us -> 0.66 us
  Pallas kernels: 0 us -> 14.7 us
  starting transfers between devices: 3.77 us -> 13.7 us
    reduce_scatter x1 -> x0, waiting for transfers between devices: 59.6 us -> none  [local(): lax.psum_scatter(partial_value.reshape(dst_blocks * tile_len, feat_width)...]
    all_gather x2 -> x0, blocking collectives: 37.5 us -> none  [the longest x1 31.5 us: local(): lax.all_gather(scaled_grads, 'col', axis=0, tiled=True)]
    scatter-add x8 -> x0, other arithmetic: 34.3 us -> none  [the longest x4 25.6 us: backward_add(): return accum_total.at[src_index].add(products)]
    unnamed x2 -> x0, blocking collectives: 30 us -> none
    all_to_all x0 -> x3, waiting for transfers between devices: none -> 28.4 us  [the longest x1 13 us: local(): dst_message = lax.all_to_all(dst_send, 'col', 0, 0, tiled=True)]
    dot_general x10 -> x0, matrix products: 25.9 us -> none  [the longest x4 17.9 us: backward_add(): jnp.einsum('kij,kif->kjf', chosen, rows[dst_index], preferred_element_typ...]
    gather x12 -> x0, local copies, waits for them, and re-layouts: 17.4 us -> none  [the longest x4 6.93 us: pick_tiles(): chosen = tile_weight[jnp.maximum(tile_ids, 0)] * keep_mask[:, None, None]]
    pallas_call x0 -> x5, Pallas kernels: none -> 14.7 us  [the longest x1 4.85 us: local(): pl.pallas_call(functools.partial(place_kernel, chunks, src_blocks), out_s...]
  transfers between devices with their start and end apart: 4 -> 3, of which waited for: 4 -> 3; matrix products, arithmetic and copies ran while one was open for 0% -> 0% of each run, Pallas kernels for 0% -> 12%
where the time goes in v1:
time: 71.3 us; the launch traced here: 70.6 us
  waiting for transfers between devices  28.4 us (40%)
  Pallas kernels  14.7 us (21%)
  starting transfers between devices  13.7 us (19%)
  blocking collectives  11.2 us (16%)
  local copies, waits for them, and re-layouts  2.01 us (3%)
    all_to_all x1, waiting for transfers between devices, local(): dst_message = lax.all_to_all(dst_send, 'col', 0, 0, tiled=True)  13 us
    all_to_all x1, waiting for transfers between devices, local(): dst_partials = lax.all_to_all(partial, 'col', 0, 0, tiled=True)  11.2 us
    all_to_all x1, blocking collectives, local(): src_message = lax.all_to_all(src_send, 'row', 0, 0, tiled=True)  11.2 us
    all_to_all x1, starting transfers between devices, local(): dst_message = lax.all_to_all(dst_send, 'col', 0, 0, tiled=True)  6.63 us
    pallas_call x1, Pallas kernels, local(): pl.pallas_call(functools.partial(place_kernel, chunks, src_blocks), out_s...  4.85 us
    all_to_all x1, waiting for transfers between devices, local(): src_partials = lax.all_to_all(back_partial, 'row', 0, 0, tiled=True)  4.21 us
    all_to_all x1, starting transfers between devices, local(): dst_partials = lax.all_to_all(partial, 'col', 0, 0, tiled=True)  3.64 us
    pallas_call x1, Pallas kernels, local(): pl.pallas_call(functools.partial(backward_kernel, own_blocks), out_shape=...  3.44 us
  transfers between devices with their start and end apart: 3, of which 3 were waited for; matrix products, arithmetic and copies ran while one was open for 0% of the time, Pallas kernels for 12%

profile of v1, /device:TPU:0, one launch (start us, length us, event | category | flops | bytes accessed | tf_op | source)
XLA Modules:
  0.0 70.6 jit_solution(4697356047857403196)
XLA Ops:
  0.6 1.3 %copy.6.list_ref = s32[4,3,32]{2,1,0:T(4,128)} copy(s32[4,3,32]{2,0,1:T(4,128)} %param.7) | data formatting | bytes 3072 | tf_op args[3]
  1.9 4.8 %place.1 = (bf16[1024,512]{1,0:T(8,128)(2,1)}, bf16[4,144,256]{2,1,0:T(8,128)(2,1)}, bf16[8,144,256]{2,1,0:T(8,128)(2,1)}) custom-call(s32[4,3,32]{2,1,0:T(4,128)} %copy.6.list_ref, bf16[128,256]{1,0:T(8,128)(2,1)} %features_ref.1, bf16[128,256]{1,0:T(8,128)(2,1)} %grads_ref.1, bf16[64,128,128]{2,1,0:T(8,128)(2,1)} %tiles_hbm.1), custom_call_target="tpu_custom_call" | custom-call | tf_op jit(solution)/shard_map/place/pallas_call | solution.py:266
  6.8 11.2 %all_to_all.20.message_ref = bf16[4,144,256]{2,1,0:T(8,128)(2,1)} all-to-all(bf16[4,144,256]{2,1,0:T(8,128)(2,1)} %get-tuple-element.9), channel_id=1, replica_groups=mesh['row'=4,'col'=8] {'row'}, dimensions={0} | all-to-all | bytes 589824 | tf_op jit(solution)/shard_map/all_to_all | solution.py:290
  18.0 6.6 %all-to-all-start.2 = ((bf16[8,144,256]{2,1,0:T(8,128)(2,1)}), bf16[8,144,256]{2,1,0:T(8,128)(2,1)S(1)}, u32[]{:S(2)}, u32[]{:S(2)}) async-start(bf16[8,144,256]{2,1,0:T(8,128)(2,1)} %get-tuple-element.12), calls=%async_computation.2 | async-start | bytes 1179648 | tf_op jit(solution)/shard_map/all_to_all | solution.py:291
  24.6 3.0 %forward.1 = (bf16[8,128,256]{2,1,0:T(8,128)(2,1)}, f32[128,128]{1,0:T(8,128)}) custom-call(bf16[4,144,256]{2,1,0:T(8,128)(2,1)} %all_to_all.20.message_ref, bf16[1024,512]{1,0:T(8,128)(2,1)} %get-tuple-element.10.adjacency_ref), custom_call_target="tpu_custom_call" | custom-call | tf_op jit(solution)/shard_map/forward/pallas_call | solution.py:292
  27.6 13.0 %all-to-all-done.2.message_ref = bf16[8,144,256]{2,1,0:T(8,128)(2,1)S(1)} async-done(((bf16[8,144,256]{2,1,0:T(8,128)(2,1)}), bf16[8,144,256]{2,1,0:T(8,128)(2,1)S(1)}, u32[]{:S(2)}, u32[]{:S(2)}) %all-to-all-start.2) | async-done | bytes 589856 | tf_op jit(solution)/shard_map/all_to_all | solution.py:291
  40.6 0.0 copy-start
  40.6 3.6 %all-to-all-start.1 = ((bf16[8,128,256]{2,1,0:T(8,128)(2,1)}), bf16[8,128,256]{2,1,0:T(8,128)(2,1)S(1)}, u32[]{:S(2)}, u32[]{:S(2)}) async-start(bf16[8,128,256]{2,1,0:T(8,128)(2,1)} %get-tuple-element.11), calls=%async_computation.1 | async-start | bytes 1048576 | tf_op jit(solution)/shard_map/all_to_all | solution.py:303
  44.2 0.0 copy-done
  44.2 3.4 %backward.1 = (bf16[4,128,256]{2,1,0:T(8,128)(2,1)}, f32[128,128]{1,0:T(8,128)}) custom-call(bf16[8,144,256]{2,1,0:T(8,128)(2,1)} %copy-done, bf16[1024,512]{1,0:T(8,128)(2,1)} %get-tuple-element.10.adjacency_ref), custom_call_target="tpu_custom_call" | custom-call | tf_op jit(solution)/shard_map/backward/pallas_call | solution.py:304
  47.7 11.2 %all-to-all-done.1.received_ref = bf16[8,128,256]{2,1,0:T(8,128)(2,1)S(1)} async-done(((bf16[8,128,256]{2,1,0:T(8,128)(2,1)}), bf16[8,128,256]{2,1,0:T(8,128)(2,1)S(1)}, u32[]{:S(2)}, u32[]{:S(2)}) %all-to-all-start.1) | async-done | bytes 524320 | tf_op jit(solution)/shard_map/all_to_all | solution.py:303
  58.9 0.0 copy-start.1
  58.9 3.4 %all-to-all-start.3 = ((bf16[4,128,256]{2,1,0:T(8,128)(2,1)}), bf16[4,128,256]{2,1,0:T(8,128)(2,1)S(1)}, u32[]{:S(2)}, u32[]{:S(2)}) async-start(bf16[4,128,256]{2,1,0:T(8,128)(2,1)} %get-tuple-element.14), calls=%async_computation.3 | async-start | bytes 524288 | tf_op jit(solution)/shard_map/all_to_all | solution.py:315
  62.3 0.0 copy-done.1
  62.3 1.8 %finish.2 = bf16[128,256]{1,0:T(8,128)(2,1)} custom-call(bf16[8,128,256]{2,1,0:T(8,128)(2,1)} %copy-done.1, f32[128,128]{1,0:T(8,128)} %get-tuple-element.13.scale_ref), custom_call_target="tpu_custom_call" | custom-call | tf_op jit(solution)/shard_map/finish/pallas_call | solution.py:318
  64.1 4.2 %all-to-all-done.3.received_ref = bf16[4,128,256]{2,1,0:T(8,128)(2,1)S(1)} async-done(((bf16[4,128,256]{2,1,0:T(8,128)(2,1)}), bf16[4,128,256]{2,1,0:T(8,128)(2,1)S(1)}, u32[]{:S(2)}, u32[]{:S(2)}) %all-to-all-start.3) | async-done | bytes 262176 | tf_op jit(solution)/shard_map/all_to_all | solution.py:315
  68.3 0.0 copy-start.2
  68.3 0.7 copy-done.2
  69.0 1.6 %finish.3 = bf16[128,256]{1,0:T(8,128)(2,1)} custom-call(bf16[4,128,256]{2,1,0:T(8,128)(2,1)} %copy-done.2, f32[128,128]{1,0:T(8,128)} %get-tuple-element.15.scale_ref), custom_call_target="tpu_custom_call" | custom-call | tf_op jit(solution)/shard_map/finish/pallas_call | solution.py:318
Async XLA Ops:
  18.0 22.6 %all-to-all-start.2 = ((bf16[8,144,256]{2,1,0:T(8,128)(2,1)}), bf16[8,144,256]{2,1,0:T(8,128)(2,1)S(1)}, u32[]{:S(2)}, u32[]{:S(2)}) async-start(bf16[8,144,256]{2,1,0:T(8,128)(2,1)} %get-tuple-element.12), calls=%async_computation.2 | async-start | bytes 1179648 | tf_op jit(solution)/shard_map/all_to_all | solution.py:291
  40.6 3.6 %copy-start = (bf16[8,144,256]{2,1,0:T(8,128)(2,1)}, bf16[8,144,256]{2,1,0:T(8,128)(2,1)S(1)}, u32[]{:S(2)}) copy-start(bf16[8,144,256]{2,1,0:T(8,128)(2,1)S(1)} %all-to-all-done.2.message_ref) | copy-start | bytes 1769476
  40.6 18.3 %all-to-all-start.1 = ((bf16[8,128,256]{2,1,0:T(8,128)(2,1)}), bf16[8,128,256]{2,1,0:T(8,128)(2,1)S(1)}, u32[]{:S(2)}, u32[]{:S(2)}) async-start(bf16[8,128,256]{2,1,0:T(8,128)(2,1)} %get-tuple-element.11), calls=%async_computation.1 | async-start | bytes 1048576 | tf_op jit(solution)/shard_map/all_to_all | solution.py:303
  58.9 3.4 %copy-start.1 = (bf16[8,128,256]{2,1,0:T(8,128)(2,1)}, bf16[8,128,256]{2,1,0:T(8,128)(2,1)S(1)}, u32[]{:S(2)}) copy-start(bf16[8,128,256]{2,1,0:T(8,128)(2,1)S(1)} %all-to-all-done.1.received_ref) | copy-start | bytes 1572868
  58.9 9.4 %all-to-all-start.3 = ((bf16[4,128,256]{2,1,0:T(8,128)(2,1)}), bf16[4,128,256]{2,1,0:T(8,128)(2,1)S(1)}, u32[]{:S(2)}, u32[]{:S(2)}) async-start(bf16[4,128,256]{2,1,0:T(8,128)(2,1)} %get-tuple-element.14), calls=%async_computation.3 | async-start | bytes 524288 | tf_op jit(solution)/shard_map/all_to_all | solution.py:315
  68.3 0.7 %copy-start.2 = (bf16[4,128,256]{2,1,0:T(8,128)(2,1)}, bf16[4,128,256]{2,1,0:T(8,128)(2,1)S(1)}, u32[]{:S(2)}) copy-start(bf16[4,128,256]{2,1,0:T(8,128)(2,1)S(1)} %all-to-all-done.3.received_ref) | copy-start | bytes 786436

commit v2 on v1

v2 whole, which is shorter than its diff:
```python
import functools

import jax
import jax.numpy as jnp
from jax import lax
from jax.experimental import pallas as pl
from jax.experimental.pallas import tpu as pltpu
from jax.sharding import PartitionSpec as P


F32 = jnp.float32
BF16 = jnp.bfloat16
PARTS = 3


def round_up(value, step):
    return -(-value // step) * step


def meet(here, k, count):
    if count & (count - 1) == 0:
        return here ^ k, here ^ k
    return lax.rem(here + k, count), lax.rem(here - k + count, count)


def exchange(value, axis, k):
    count = lax.axis_size(axis)
    if count & (count - 1) == 0:
        pairs = [(source, source ^ k) for source in range(count)]
    else:
        pairs = [(source, (source + k) % count) for source in range(count)]
    return lax.ppermute(value, axis, pairs)


def message_rows(count, width):
    part_rows = count // width
    return part_rows, round_up(PARTS * part_rows, 16)


def pack_counts(counts, width):
    rows, total = counts.shape
    part_rows = total // width
    row = lax.broadcasted_iota(jnp.int32, (rows, width), 0)
    value = jnp.zeros((rows, width), F32)
    for i in range(part_rows):
        here = row == i
        for part in range(1, PARTS):
            here = here | (row == part * part_rows + i)
        value = jnp.where(here, counts[:, i * width : (i + 1) * width], value)
    high = value.astype(BF16).astype(F32)
    middle = (value - high).astype(BF16).astype(F32)
    low = value - high - middle
    packed = jnp.where(row < part_rows, high, jnp.where(row < 2 * part_rows, middle, low))
    return packed.astype(BF16)


def scale_rows(messages, places, tile_len, scales_ref, scaled_ref, own_scale_ref):
    senders = len(messages)
    width = messages[0].shape[1]
    body = own_scale_ref.shape[0]
    part_rows = senders * body // width
    parts = messages[0][body:].astype(F32)
    for message_ref in messages[1:]:
        parts = parts + message_ref[body:].astype(F32)
    total = parts[0:part_rows]
    for part in range(1, PARTS):
        total = total + parts[part * part_rows : (part + 1) * part_rows]
    scales = lax.rsqrt(1.0 + total)
    for block in range(senders * body // tile_len):
        row, first = divmod(block * tile_len, width)
        scales_ref[block : block + 1] = scales[row : row + 1, first : first + tile_len]
    for index, (message_ref, place) in enumerate(zip(messages, places)):
        for b in range(body // tile_len):
            block = place * (body // tile_len) + b
            line = scales_ref[pl.ds(block, 1)]
            column = jnp.broadcast_to(line, (tile_len, tile_len)).T
            rows_here = message_ref[b * tile_len : (b + 1) * tile_len]
            first = pl.multiple_of(block * tile_len, tile_len)
            scaled_ref[pl.ds(first, tile_len)] = scaled_rows(rows_here, column).astype(BF16)
            if index == 0:
                own_scale_ref[b * tile_len : (b + 1) * tile_len] = column


def scaled_rows(rows, column):
    width = rows.shape[1]
    tile_len = column.shape[1]
    pieces = [
        rows[:, i * tile_len : (i + 1) * tile_len].astype(F32) * column
        for i in range(width // tile_len)
    ]
    return jnp.concatenate(pieces, axis=1)


def place_kernel(
    chunks,
    src_blocks,
    list_hbm,
    features_hbm,
    grads_hbm,
    tiles_hbm,
    adjacency_ref,
    src_send_ref,
    dst_send_ref,
    tiles_ref,
    total_ref,
    line_ref,
    list_ref,
    where_ref,
    sems,
):
    tile_count, tile_len, _ = tiles_ref.shape
    _, step_count, slot_count = list_ref.shape
    width = features_hbm.shape[1]
    dst_blocks = adjacency_ref.shape[0] // tile_len
    slots = adjacency_ref.shape[1] // tile_len
    pairs = dst_blocks * slots
    per_chunk = tile_count // chunks

    def chunk_copy(i):
        window = pl.ds(i * per_chunk, per_chunk)
        return pltpu.make_async_copy(tiles_hbm.at[window], tiles_ref.at[window], sems.at[i])

    list_copy = pltpu.make_async_copy(list_hbm, list_ref, sems.at[chunks])
    row_copies = [
        pltpu.make_async_copy(
            features_hbm, src_send_ref.at[pl.ds(0, features_hbm.shape[0])], sems.at[chunks + 1]
        ),
        pltpu.make_async_copy(
            grads_hbm, dst_send_ref.at[pl.ds(0, grads_hbm.shape[0])], sems.at[chunks + 2]
        ),
    ]
    list_copy.start()
    for i in range(chunks):
        chunk_copy(i).start()
    for copy in row_copies:
        copy.start()

    @pl.loop(0, pairs + 1)
    def _(p):
        total_ref[p] = jnp.zeros((tile_len, tile_len), F32)

    @pl.loop(0, tile_count, unroll=8 if tile_count % 8 == 0 else 1)
    def _(t):
        where_ref[t] = pairs

    list_copy.wait()
    row_pos = lax.axis_index("row")
    for step in range(step_count):
        first = lax.rem(row_pos - step + step_count, step_count) * src_blocks

        @pl.loop(0, slot_count, unroll=8 if slot_count % 8 == 0 else 1)
        def _(k):
            t = list_ref[0, step, k]
            pair = list_ref[2, step, k] * slots + first + list_ref[1, step, k]
            where_ref[jnp.where(t >= 0, t, tile_count)] = pair

    for i in range(chunks):
        chunk_copy(i).wait()

        @pl.loop(i * per_chunk, (i + 1) * per_chunk, unroll=4 if per_chunk % 4 == 0 else 1)
        def _(t):
            p = where_ref[t]
            total_ref[p] = total_ref[p] + tiles_ref[t].astype(F32)

    src_rows = src_send_ref.shape[0] - features_hbm.shape[0]
    dst_rows = dst_send_ref.shape[0] - grads_hbm.shape[0]
    col_sums = tuple(jnp.zeros((8, tile_len), F32) for _ in range(slots))

    def block_row(e, sums):
        first = pl.multiple_of(e * tile_len, tile_len)
        across = jnp.zeros((tile_len, tile_len), F32)
        out = []
        for s in range(slots):
            block = total_ref[e * slots + s]
            adjacency_ref[pl.ds(first, tile_len), s * tile_len : (s + 1) * tile_len] = block.astype(
                BF16
            )
            across = across + block
            out.append(sums[s] + jnp.sum(block.reshape(tile_len // 8, 8, tile_len), axis=0))
        high = across.astype(BF16)
        low = (across - high.astype(F32)).astype(BF16)
        ones = jnp.ones((dst_rows, tile_len), BF16)
        contract = (((1,), (1,)), ((), ()))
        line_ref[:, pl.ds(first, tile_len)] = lax.dot_general(
            ones, high, contract, preferred_element_type=F32
        ) + lax.dot_general(ones, low, contract, preferred_element_type=F32)
        return tuple(out)

    if dst_blocks <= 8:
        for e in range(dst_blocks):
            col_sums = block_row(e, col_sums)
    else:
        col_sums = lax.fori_loop(0, dst_blocks, block_row, col_sums)
    src_line = jnp.concatenate(
        [
            jnp.broadcast_to(jnp.sum(sums, axis=0, keepdims=True), (src_rows, tile_len))
            for sums in col_sums
        ],
        axis=1,
    )
    src_packed = pack_counts(src_line, width)
    dst_packed = pack_counts(line_ref[...], width)
    src_send_ref[features_hbm.shape[0] :] = src_packed
    dst_send_ref[grads_hbm.shape[0] :] = dst_packed
    for copy in row_copies:
        copy.wait()


def forward_kernel(senders, receivers, own_rows, *refs):
    messages, adjacency_ref = refs[:senders], refs[senders]
    partial_refs = refs[senders + 1 : senders + 1 + receivers]
    own_scale_ref, scales_ref, scaled_ref = refs[senders + 1 + receivers :]
    rows = partial_refs[0].shape[0]
    row_pos = lax.axis_index("row")
    places = [meet(row_pos, k, senders)[1] for k in range(senders)]
    scale_rows(messages, places, own_scale_ref.shape[1], scales_ref, scaled_ref, own_scale_ref)
    col_pos = lax.axis_index("col")
    for k, partial_ref in enumerate(partial_refs):
        near = meet(col_pos, k, receivers)[0]
        for half in range(rows // own_rows):
            block = near ^ receivers if half else near
            first = pl.multiple_of(block * own_rows, own_rows)
            partial_ref[half * own_rows : (half + 1) * own_rows] = jnp.dot(
                adjacency_ref[pl.ds(first, own_rows)], scaled_ref[...], preferred_element_type=F32
            ).astype(partial_ref.dtype)


def backward_kernel(senders, receivers, halves, *refs):
    messages, adjacency_ref = refs[:senders], refs[senders]
    partial_refs = refs[senders + 1 : senders + 1 + receivers]
    own_scale_ref, scales_ref, scaled_ref = refs[senders + 1 + receivers :]
    src_rows = partial_refs[0].shape[0]
    group = senders // halves
    col_pos = lax.axis_index("col")
    places = [meet(col_pos, k, group)[1] for k in range(group)]
    if halves == 2:
        places = places + [place ^ group for place in places]
    scale_rows(messages, places, own_scale_ref.shape[1], scales_ref, scaled_ref, own_scale_ref)
    row_pos = lax.axis_index("row")
    for k, partial_ref in enumerate(partial_refs):
        first = pl.multiple_of(meet(row_pos, k, receivers)[0] * src_rows, src_rows)
        partial_ref[...] = lax.dot_general(
            adjacency_ref[:, pl.ds(first, src_rows)],
            scaled_ref[...],
            (((0,), (0,)), ((), ())),
            preferred_element_type=F32,
        ).astype(partial_ref.dtype)


def merge_kernel(*refs):
    *pieces, near_ref, far_ref = refs
    rows = near_ref.shape[0]
    for half, out_ref in enumerate((near_ref, far_ref)):
        window = slice(half * rows, (half + 1) * rows)
        total = pieces[0][window].astype(F32)
        for piece in pieces[1:]:
            total = total + piece[window].astype(F32)
        out_ref[...] = total.astype(out_ref.dtype)


def finish_kernel(*refs):
    *pieces, scale_ref, out_ref = refs
    width = out_ref.shape[1]
    tile_len = scale_ref.shape[1]
    terms = []
    for piece in pieces:
        terms += [piece[...]] if len(piece.shape) == 2 else [piece[j] for j in range(piece.shape[0])]
    total = terms[0].astype(F32)
    for term in terms[1:]:
        total = total + term.astype(F32)
    column = scale_ref[...]
    for i in range(width // tile_len):
        lanes = slice(i * tile_len, (i + 1) * tile_len)
        out_ref[:, lanes] = (total[:, lanes] * column).astype(BF16)


def room(size):
    return pltpu.CompilerParams(vmem_limit_bytes=min(size + (4 << 20), 60 * 1024 * 1024))


VMEM = pl.BlockSpec(memory_space=pltpu.VMEM)


def aggregate(features, grad_out, tile_weight, tile_list):
    row_count = lax.axis_size("row")
    col_count = lax.axis_size("col")
    tile_count, tile_len, _ = tile_weight.shape
    width = features.shape[1]
    src_blocks = features.shape[0] // tile_len
    own_blocks = grad_out.shape[0] // tile_len
    slots = row_count * src_blocks
    dst_blocks = col_count * own_blocks
    _, src_rows = message_rows(slots * tile_len, width)
    _, dst_rows = message_rows(dst_blocks * tile_len, width)
    chunks = 4 if tile_count % 4 == 0 else 1
    shape = jax.ShapeDtypeStruct
    block = tile_len * tile_len
    dense = dst_blocks * slots * block
    rows_in = (slots + 2 * dst_blocks) * tile_len * width
    FORWARD = 3 * dense + 8 * rows_in
    BACKWARD = 3 * dense + 8 * rows_in
    FINISH = 4 * rows_in

    adjacency, src_send, dst_send = pl.pallas_call(
        functools.partial(place_kernel, chunks, src_blocks),
        out_shape=(
            shape((dst_blocks * tile_len, slots * tile_len), BF16),
            shape((features.shape[0] + src_rows, width), BF16),
            shape((grad_out.shape[0] + dst_rows, width), BF16),
        ),
        in_specs=[pl.BlockSpec(memory_space=pltpu.HBM)] * 4,
        out_specs=(VMEM, VMEM, VMEM),
        scratch_shapes=[
            pltpu.VMEM((tile_count, tile_len, tile_len), BF16),
            pltpu.VMEM((dst_blocks * slots + 1, tile_len, tile_len), F32),
            pltpu.VMEM((dst_rows, dst_blocks * tile_len), F32),
            pltpu.SMEM((tile_list.shape[1], row_count, tile_list.shape[2]), jnp.int32),
            pltpu.SMEM((tile_count + 1,), jnp.int32),
            pltpu.SemaphoreType.DMA((chunks + 3,)),
        ],
        compiler_params=room(60 * 1024 * 1024),
        name="place",
    )(jnp.transpose(tile_list, (1, 0, 2)), features, grad_out, tile_weight)

    own_rows = grad_out.shape[0]
    halves = 2 if col_count >= 4 and col_count & (col_count - 1) == 0 else 1
    group = col_count // halves

    def near(value, k):
        if halves == 1:
            return exchange(value, "col", k)
        return lax.ppermute(value, "col", [(c, c ^ k) for c in range(col_count)])

    src_messages = [src_send] + [exchange(src_send, "row", k) for k in range(1, row_count)]
    if halves == 2:
        far_send = exchange(dst_send, "col", group)
    dst_messages = [dst_send] + [near(dst_send, k) for k in range(1, group)]
    if halves == 2:
        dst_messages += [far_send] + [near(far_send, k) for k in range(1, group)]

    *partials, src_scale = pl.pallas_call(
        functools.partial(forward_kernel, row_count, group, own_rows),
        out_shape=(
            *(shape((halves * own_rows, width), BF16 if k else F32) for k in range(group)),
            shape((features.shape[0], tile_len), F32),
        ),
        in_specs=[VMEM] * (row_count + 1),
        out_specs=(VMEM,) * (group + 1),
        scratch_shapes=[
            pltpu.VMEM((slots, tile_len), F32),
            pltpu.VMEM((slots * tile_len, width), BF16),
        ],
        compiler_params=room(FORWARD),
        name="forward",
    )(*src_messages, adjacency)
    dst_partials = partials[:1] + [near(partials[k], k) for k in range(1, group)]
    if halves == 2:
        kept, sent = pl.pallas_call(
            merge_kernel,
            out_shape=(shape((own_rows, width), F32), shape((own_rows, width), BF16)),
            in_specs=[VMEM] * group,
            out_specs=(VMEM, VMEM),
            compiler_params=room(FINISH),
            name="merge",
        )(*dst_partials)
        dst_partials = [kept, exchange(sent, "col", group)]
    *back_partials, dst_scale = pl.pallas_call(
        functools.partial(backward_kernel, col_count, row_count, halves),
        out_shape=(
            *(
                shape((features.shape[0], width), BF16 if k else F32)
                for k in range(row_count)
            ),
            shape((grad_out.shape[0], tile_len), F32),
        ),
        in_specs=[VMEM] * (col_count + 1),
        out_specs=(VMEM,) * (row_count + 1),
        scratch_shapes=[
            pltpu.VMEM((dst_blocks, tile_len), F32),
            pltpu.VMEM((dst_blocks * tile_len, width), BF16),
        ],
        compiler_params=room(BACKWARD),
        name="backward",
    )(*dst_messages, adjacency)
    src_partials = back_partials[:1] + [
        exchange(back_partials[k], "row", k) for k in range(1, row_count)
    ]

    def finish(received, scale, rows):
        return pl.pallas_call(
            finish_kernel,
            out_shape=shape((rows, width), BF16),
            in_specs=[VMEM] * (len(received) + 1),
            out_specs=VMEM,
            compiler_params=room(FINISH),
            name="finish",
        )(*received, scale)

    feature_grad = finish(src_partials, src_scale, features.shape[0])
    aggregated = finish(dst_partials, dst_scale, grad_out.shape[0])
    return (aggregated, feature_grad)


def solution(mesh):
    return jax.shard_map(
        aggregate,
        mesh=mesh,
        in_specs=(
            P(("row", "col"), None),
            P(("row", "col"), None),
            P(("row", "col"), None, None),
            P(("row", "col"), None, None),
        ),
        out_specs=(P(("row", "col"), None), P(("row", "col"), None)),
        check_vma=False,
    )
```

time: 71.3 us -> 42.2 us (0.59)
  waiting for transfers between devices: 28.4 us -> 11.5 us
  blocking collectives: 11.2 us -> 0 us
  Pallas kernels: 14.7 us -> 6.2 us
  starting transfers between devices: 13.7 us -> 20.6 us
  local copies, waits for them, and re-layouts: 2.01 us -> 2.99 us
    all_to_all x3 -> x0, waiting for transfers between devices: 28.4 us -> none  [the longest x1 13 us: local(): dst_message = lax.all_to_all(dst_send, 'col', 0, 0, tiled=True)]
    ppermute x0 -> x17, starting transfers between devices: none -> 20.6 us  [the longest x9 10.5 us: near(): return lax.ppermute(value, 'col', [(c, c ^ k) for c in range(col_count)])]
    all_to_all x3 -> x0, starting transfers between devices: 13.7 us -> none  [the longest x1 6.63 us: local(): dst_message = lax.all_to_all(dst_send, 'col', 0, 0, tiled=True)]
    ppermute x0 -> x17, waiting for transfers between devices: none -> 11.5 us  [the longest x9 6.82 us: near(): return lax.ppermute(value, 'col', [(c, c ^ k) for c in range(col_count)])]
    all_to_all x1 -> x0, blocking collectives: 11.2 us -> none  [local(): src_message = lax.all_to_all(src_send, 'row', 0, 0, tiled=True)]
    pallas_call x3 -> x4, Pallas kernels: 11.3 us -> 4.88 us  [the longest x1 3.53 us: aggregate(): pl.pallas_call(functools.partial(place_kernel, chunks, src_blocks), out_s...]
    pallas_call x2, Pallas kernels: 3.38 us -> 1.32 us  [finish(): pl.pallas_call(finish_kernel, out_shape=shape((rows, width), BF16), in_sp...]
    unnamed x7 -> x6, local copies, waits for them, and re-layouts: 2.01 us -> 2.99 us
  transfers between devices with their start and end apart: 3 -> 17, of which waited for: 3 -> 6; matrix products, arithmetic and copies ran while one was open for 0% -> 0% of each run, Pallas kernels for 12% -> 5%
where the time goes in v2:
time: 42.2 us; the launch traced here: 41.9 us
  starting transfers between devices  20.6 us (49%)
  waiting for transfers between devices  11.5 us (27%)
  Pallas kernels  6.2 us (15%)
  local copies, waits for them, and re-layouts  2.99 us (7%)
  between operations  0.69 us (2%)
    ppermute x9, starting transfers between devices, near(): return lax.ppermute(value, 'col', [(c, c ^ k) for c in range(col_count)])  10.5 us
    ppermute x8, starting transfers between devices, exchange(): return lax.ppermute(value, axis, pairs)  10 us
    ppermute x9, waiting for transfers between devices, near(): return lax.ppermute(value, 'col', [(c, c ^ k) for c in range(col_count)])  6.82 us
    ppermute x8, waiting for transfers between devices, exchange(): return lax.ppermute(value, axis, pairs)  4.63 us
    pallas_call x1, Pallas kernels, aggregate(): pl.pallas_call(functools.partial(place_kernel, chunks, src_blocks), out_s...  3.53 us
    unnamed x6, local copies, waits for them, and re-layouts  2.99 us
    pallas_call x2, Pallas kernels, finish(): pl.pallas_call(finish_kernel, out_shape=shape((rows, width), BF16), in_sp...  1.32 us
  transfers between devices with their start and end apart: 17, of which 6 were waited for; matrix products, arithmetic and copies ran while one was open for 0% of the time, Pallas kernels for 5%

profile of v2, /device:TPU:0, one launch (start us, length us, event | category | flops | bytes accessed | tf_op | source)
XLA Modules:
  0.0 41.9 jit_solution(14236925732955204618)
XLA Ops:
  0.6 3.5 %place.1 = (bf16[1024,512]{1,0:T(8,128)(2,1)}, bf16[144,256]{1,0:T(8,128)(2,1)}, bf16[144,256]{1,0:T(8,128)(2,1)}) custom-call(s32[3,4,32]{2,1,0:T(4,128)} %bitcast.1, bf16[128,256]{1,0:T(8,128)(2,1)} %features_hbm.1, bf16[128,256]{1,0:T(8,128)(2,1)} %grads_hbm.1, bf16[64,128,128]{2,1,0:T(8,128)(2,1)} %tiles_hbm.1), custom_call_target="tpu_custom_call" | custom-call | tf_op jit(solution)/shard_map/place/pallas_call | solution.py:304
  4.2 0.5 %collective-permute-start = (bf16[144,256]{1,0:T(8,128)(2,1)}, bf16[144,256]{1,0:T(8,128)(2,1)S(1)}, u32[]{:S(2)}, u32[]{:S(2)}) collective-permute-start(bf16[144,256]{1,0:T(8,128)(2,1)} %get-tuple-element.17.refs_0_), channel_id=1, source_target_pairs={{0,8},{8,0},{16,24},{24,16},{1,9},{9,1},{17,25},{25,17},{2,10},{10... | collective-permute-start | bytes 221192 | tf_op jit(solution)/shard_map/ppermute | solution.py:32
  4.7 2.6 %collective-permute-start.1 = (bf16[144,256]{1,0:T(8,128)(2,1)}, bf16[144,256]{1,0:T(8,128)(2,1)S(1)}, u32[]{:S(2)}, u32[]{:S(2)}) collective-permute-start(bf16[144,256]{1,0:T(8,128)(2,1)} %get-tuple-element.17.refs_0_), channel_id=1, source_target_pairs={{0,16},{8,24},{16,0},{24,8},{1,17},{9,25},{17,1},{25,9},{2,18},{10... | collective-permute-start | bytes 221192 | tf_op jit(solution)/shard_map/ppermute | solution.py:32
  7.3 2.6 %collective-permute-start.10 = (bf16[144,256]{1,0:T(8,128)(2,1)}, bf16[144,256]{1,0:T(8,128)(2,1)S(1)}, u32[]{:S(2)}, u32[]{:S(2)}) collective-permute-start(bf16[144,256]{1,0:T(8,128)(2,1)} %get-tuple-element.25.refs_0_), channel_id=1, source_target_pairs={{0,4},{1,5},{2,6},{3,7},{4,0},{5,1},{6,2},{7,3},{8,12},{9,13},{10,... | collective-permute-start | bytes 221192 | tf_op jit(solution)/shard_map/ppermute | solution.py:32
  9.9 0.0 collective-permute-start.2
  9.9 1.5 %collective-permute-start.7 = (bf16[144,256]{1,0:T(8,128)(2,1)}, bf16[144,256]{1,0:T(8,128)(2,1)S(1)}, u32[]{:S(2)}, u32[]{:S(2)}) collective-permute-start(bf16[144,256]{1,0:T(8,128)(2,1)} %get-tuple-element.25.refs_0_), channel_id=1, source_target_pairs={{0,1},{1,0},{2,3},{3,2},{4,5},{5,4},{6,7},{7,6},{8,9},{9,8},{10,11... | collective-permute-start | bytes 221192 | tf_op jit(solution)/shard_map/ppermute | solution.py:332
  11.4 0.0 collective-permute-done.refs_1_
  11.4 1.6 %collective-permute-start.8 = (bf16[144,256]{1,0:T(8,128)(2,1)}, bf16[144,256]{1,0:T(8,128)(2,1)S(1)}, u32[]{:S(2)}, u32[]{:S(2)}) collective-permute-start(bf16[144,256]{1,0:T(8,128)(2,1)} %get-tuple-element.25.refs_0_), channel_id=1, source_target_pairs={{0,2},{1,3},{2,0},{3,1},{4,6},{5,7},{6,4},{7,5},{8,10},{9,11},{10,... | collective-permute-start | bytes 221192 | tf_op jit(solution)/shard_map/ppermute | solution.py:332
  13.0 0.0 collective-permute-done.1.refs_2_
  13.0 0.4 collective-permute-start.9
  13.4 1.0 %collective-permute-done.10.refs_4_ = bf16[144,256]{1,0:T(8,128)(2,1)S(1)} collective-permute-done((bf16[144,256]{1,0:T(8,128)(2,1)}, bf16[144,256]{1,0:T(8,128)(2,1)S(1)}, u32[]{:S(2)}, u32[]{:S(2)}) %collective-permute-start.10) | collective-permute-done | bytes 73760 | tf_op jit(solution)/shard_map/ppermute | solution.py:32
  14.4 1.4 %collective-permute-start.11 = (bf16[144,256]{1,0:T(8,128)(2,1)S(1)}, bf16[144,256]{1,0:T(8,128)(2,1)S(1)}, u32[]{:S(2)}, u32[]{:S(2)}) collective-permute-start(bf16[144,256]{1,0:T(8,128)(2,1)S(1)} %collective-permute-done.10.refs_4_), channel_id=1, source_target_pairs={{0,1},{1,0},{2,3},{3,2},{4,5},{5,4},{6,7},{7,6},{8,9},{9,8},{10,11... | collective-permute-start | bytes 221192 | tf_op jit(solution)/shard_map/ppermute | solution.py:332
  15.8 0.0 collective-permute-done.2.refs_3_
  15.8 0.0 copy-start
  15.8 1.2 %copy-done = bf16[1024,512]{1,0:T(8,128)(2,1)S(1)} copy-done((bf16[1024,512]{1,0:T(8,128)(2,1)S(1)}, bf16[1024,512]{1,0:T(8,128)(2,1)}, u32[]{:S(2)}) %copy-start) | copy-done | bytes 1048600
  17.0 0.0 copy-start.2
  17.0 0.9 %copy-done.2 = bf16[144,256]{1,0:T(8,128)(2,1)S(1)} copy-done((bf16[144,256]{1,0:T(8,128)(2,1)S(1)}, bf16[144,256]{1,0:T(8,128)(2,1)}, u32[]{:S(2)}) %copy-start.2) | copy-done | bytes 73752
  17.9 0.6 %forward.1 = (f32[256,256]{1,0:T(8,128)S(1)}, bf16[256,256]{1,0:T(8,128)(2,1)S(1)}, bf16[256,256]{1,0:T(8,128)(2,1)S(1)}, bf16[256,256]{1,0:T(8,128)(2,1)S(1)}, f32[128,128]{1,0:T(8,128)S(1)}) custom-call(bf16[144,256]{1,0:T(8,128)(2,1)S(1)} %copy-done.2, bf16[144,256]{1,0:T(8,128)(2,1)S(1)} %collective-permute-done.refs_1_, ...), custom_call_target="tpu_custom_call" | custom-call | tf_op jit(solution)/shard_map/forward/pallas_call | solution.py:341
  18.5 0.7 %collective-permute-start.3 = (bf16[256,256]{1,0:T(8,128)(2,1)S(1)}, bf16[256,256]{1,0:T(8,128)(2,1)S(1)}, u32[]{:S(2)}, u32[]{:S(2)}) collective-permute-start(bf16[256,256]{1,0:T(8,128)(2,1)S(1)} %get-tuple-element.20), channel_id=1, source_target_pairs={{0,1},{1,0},{2,3},{3,2},{4,5},{5,4},{6,7},{7,6},{8,9},{9,8},{10,11... | collective-permute-start | bytes 393224 | tf_op jit(solution)/shard_map/ppermute | solution.py:332
  19.2 0.0 collective-permute-done.7.refs_1_
  19.2 1.3 %collective-permute-start.4 = (bf16[256,256]{1,0:T(8,128)(2,1)S(1)}, bf16[256,256]{1,0:T(8,128)(2,1)S(1)}, u32[]{:S(2)}, u32[]{:S(2)}) collective-permute-start(bf16[256,256]{1,0:T(8,128)(2,1)S(1)} %get-tuple-element.21), channel_id=1, source_target_pairs={{0,2},{1,3},{2,0},{3,1},{4,6},{5,7},{6,4},{7,5},{8,10},{9,11},{10,... | collective-permute-start | bytes 393224 | tf_op jit(solution)/shard_map/ppermute | solution.py:332
  20.5 0.0 collective-permute-done.8.refs_2_
  20.5 1.6 %collective-permute-start.5 = (bf16[256,256]{1,0:T(8,128)(2,1)S(1)}, bf16[256,256]{1,0:T(8,128)(2,1)S(1)}, u32[]{:S(2)}, u32[]{:S(2)}) collective-permute-start(bf16[256,256]{1,0:T(8,128)(2,1)S(1)} %get-tuple-element.22), channel_id=1, source_target_pairs={{0,3},{1,2},{2,1},{3,0},{4,7},{5,6},{6,5},{7,4},{8,11},{9,10},{10,... | collective-permute-start | bytes 393224 | tf_op jit(solution)/shard_map/ppermute | solution.py:332
  22.0 0.0 collective-permute-done.9.refs_3_
  22.0 0.9 %collective-permute-start.12 = (bf16[144,256]{1,0:T(8,128)(2,1)S(1)}, bf16[144,256]{1,0:T(8,128)(2,1)S(1)}, u32[]{:S(2)}, u32[]{:S(2)}) collective-permute-start(bf16[144,256]{1,0:T(8,128)(2,1)S(1)} %collective-permute-done.10.refs_4_), channel_id=1, source_target_pairs={{0,2},{1,3},{2,0},{3,1},{4,6},{5,7},{6,4},{7,5},{8,10},{9,11},{10,... | collective-permute-start | bytes 221192 | tf_op jit(solution)/shard_map/ppermute | solution.py:332
  22.9 0.0 collective-permute-done.11.refs_5_
  22.9 1.2 %collective-permute-start.13 = (bf16[144,256]{1,0:T(8,128)(2,1)S(1)}, bf16[144,256]{1,0:T(8,128)(2,1)S(1)}, u32[]{:S(2)}, u32[]{:S(2)}) collective-permute-start(bf16[144,256]{1,0:T(8,128)(2,1)S(1)} %collective-permute-done.10.refs_4_), channel_id=1, source_target_pairs={{0,3},{1,2},{2,1},{3,0},{4,7},{5,6},{6,5},{7,4},{8,11},{9,10},{10,... | collective-permute-start | bytes 221192 | tf_op jit(solution)/shard_map/ppermute | solution.py:332
  24.1 5.2 %collective-permute-done.12.refs_6_ = bf16[144,256]{1,0:T(8,128)(2,1)S(1)} collective-permute-done((bf16[144,256]{1,0:T(8,128)(2,1)S(1)}, bf16[144,256]{1,0:T(8,128)(2,1)S(1)}, u32[]{:S(2)}, u32[]{:S(2)}) %collective-permute-start.12) | collective-permute-done | bytes 73760 | tf_op jit(solution)/shard_map/ppermute | solution.py:332
  29.4 1.6 %collective-permute-done.13.refs_7_ = bf16[144,256]{1,0:T(8,128)(2,1)S(1)} collective-permute-done((bf16[144,256]{1,0:T(8,128)(2,1)S(1)}, bf16[144,256]{1,0:T(8,128)(2,1)S(1)}, u32[]{:S(2)}, u32[]{:S(2)}) %collective-permute-start.13) | collective-permute-done | bytes 73760 | tf_op jit(solution)/shard_map/ppermute | solution.py:332
  30.9 0.0 copy-start.1
  30.9 0.9 %copy-done.1 = bf16[144,256]{1,0:T(8,128)(2,1)S(1)} copy-done((bf16[144,256]{1,0:T(8,128)(2,1)S(1)}, bf16[144,256]{1,0:T(8,128)(2,1)}, u32[]{:S(2)}) %copy-start.1) | copy-done | bytes 73752
  31.8 0.7 %backward.1 = (f32[128,256]{1,0:T(8,128)S(1)}, bf16[128,256]{1,0:T(8,128)(2,1)S(1)}, bf16[128,256]{1,0:T(8,128)(2,1)S(1)}, bf16[128,256]{1,0:T(8,128)(2,1)S(1)}, f32[128,128]{1,0:T(8,128)S(1)}) custom-call(bf16[144,256]{1,0:T(8,128)(2,1)S(1)} %copy-done.1, bf16[144,256]{1,0:T(8,128)(2,1)S(1)} %collective-permute-done.7.refs_1_, ...), custom_call_target="tpu_custom_call" | custom-call | tf_op jit(solution)/shard_map/backward/pallas_call | solution.py:367
  32.5 0.1 collective-permute-start.14
  32.6 0.6 %collective-permute-start.15 = (bf16[128,256]{1,0:T(8,128)(2,1)S(1)}, bf16[128,256]{1,0:T(8,128)(2,1)S(1)}, u32[]{:S(2)}, u32[]{:S(2)}) collective-permute-start(bf16[128,256]{1,0:T(8,128)(2,1)S(1)} %get-tuple-element.29), channel_id=1, source_target_pairs={{0,16},{8,24},{16,0},{24,8},{1,17},{9,25},{17,1},{25,9},{2,18},{10... | collective-permute-start | bytes 196616 | tf_op jit(solution)/shard_map/ppermute | solution.py:32
  33.2 0.0 collective-permute-done.3.refs_1_
  33.2 1.2 %collective-permute-start.16 = (bf16[128,256]{1,0:T(8,128)(2,1)S(1)}, bf16[128,256]{1,0:T(8,128)(2,1)S(1)}, u32[]{:S(2)}, u32[]{:S(2)}) collective-permute-start(bf16[128,256]{1,0:T(8,128)(2,1)S(1)} %get-tuple-element.30), channel_id=1, source_target_pairs={{0,24},{8,16},{16,8},{24,0},{1,25},{9,17},{17,9},{25,1},{2,26},{10... | collective-permute-start | bytes 196616 | tf_op jit(solution)/shard_map/ppermute | solution.py:32
  34.5 0.0 collective-permute-done.4.refs_2_
  34.5 0.0 collective-permute-done.5.refs_3_
  34.5 0.1 merge.1
  34.5 2.4 %collective-permute-start.6 = (bf16[128,256]{1,0:T(8,128)(2,1)S(1)}, bf16[128,256]{1,0:T(8,128)(2,1)S(1)}, u32[]{:S(2)}, u32[]{:S(2)}) collective-permute-start(bf16[128,256]{1,0:T(8,128)(2,1)S(1)} %get-tuple-element.24), channel_id=1, source_target_pairs={{0,4},{1,5},{2,6},{3,7},{4,0},{5,1},{6,2},{7,3},{8,12},{9,13},{10,... | collective-permute-start | bytes 196616 | tf_op jit(solution)/shard_map/ppermute | solution.py:32
  36.9 0.0 collective-permute-done.14.refs_1_
  36.9 0.7 %collective-permute-done.15.refs_2_ = bf16[128,256]{1,0:T(8,128)(2,1)S(1)} collective-permute-done((bf16[128,256]{1,0:T(8,128)(2,1)S(1)}, bf16[128,256]{1,0:T(8,128)(2,1)S(1)}, u32[]{:S(2)}, u32[]{:S(2)}) %collective-permute-start.15) | collective-permute-done | bytes 65568 | tf_op jit(solution)/shard_map/ppermute | solution.py:32
  37.6 0.3 collective-permute-done.16.refs_3_
  38.0 0.7 %finish.3 = bf16[128,256]{1,0:T(8,128)(2,1)} custom-call(f32[128,256]{1,0:T(8,128)S(1)} %get-tuple-element.27.refs_0_, bf16[128,256]{1,0:T(8,128)(2,1)S(1)} %collective-permute-done.14.refs_1_, bf16[128,256]{1,0:T(8,128)(2,1)S(1)} %collective-permute-done.15.refs_2_, bf16[128,256]{1,0:T(8,128)(2,1)S(1)} %collective-permute-done.16.refs_3_, ...), custom_call_target="tpu_custom_call" | custom-call | tf_op jit(solution)/shard_map/finish/pallas_call | solution.py:390
  38.6 2.6 %collective-permute-done.6.refs_1_ = bf16[128,256]{1,0:T(8,128)(2,1)S(1)} collective-permute-done((bf16[128,256]{1,0:T(8,128)(2,1)S(1)}, bf16[128,256]{1,0:T(8,128)(2,1)S(1)}, u32[]{:S(2)}, u32[]{:S(2)}) %collective-permute-start.6) | collective-permute-done | bytes 65568 | tf_op jit(solution)/shard_map/ppermute | solution.py:32
  41.2 0.7 %finish.2 = bf16[128,256]{1,0:T(8,128)(2,1)} custom-call(f32[128,256]{1,0:T(8,128)S(1)} %get-tuple-element.23.refs_0_, bf16[128,256]{1,0:T(8,128)(2,1)S(1)} %collective-permute-done.6.refs_1_, f32[128,128]{1,0:T(8,128)S(1)} %get-tuple-element.26.refs_2_), custom_call_target="tpu_custom_call" | custom-call | tf_op jit(solution)/shard_map/finish/pallas_call | solution.py:390
Async XLA Ops:
  4.2 7.2 %collective-permute-start = (bf16[144,256]{1,0:T(8,128)(2,1)}, bf16[144,256]{1,0:T(8,128)(2,1)S(1)}, u32[]{:S(2)}, u32[]{:S(2)}) collective-permute-start(bf16[144,256]{1,0:T(8,128)(2,1)} %get-tuple-element.17.refs_0_), channel_id=1, source_target_pairs={{0,8},{8,0},{16,24},{24,16},{1,9},{9,1},{17,25},{25,17},{2,10},{10... | collective-permute-start | bytes 221192 | tf_op jit(solution)/shard_map/ppermute | solution.py:32
  4.7 8.3 %collective-permute-start.1 = (bf16[144,256]{1,0:T(8,128)(2,1)}, bf16[144,256]{1,0:T(8,128)(2,1)S(1)}, u32[]{:S(2)}, u32[]{:S(2)}) collective-permute-start(bf16[144,256]{1,0:T(8,128)(2,1)} %get-tuple-element.17.refs_0_), channel_id=1, source_target_pairs={{0,16},{8,24},{16,0},{24,8},{1,17},{9,25},{17,1},{25,9},{2,18},{10... | collective-permute-start | bytes 221192 | tf_op jit(solution)/shard_map/ppermute | solution.py:32
  7.3 7.0 %collective-permute-start.10 = (bf16[144,256]{1,0:T(8,128)(2,1)}, bf16[144,256]{1,0:T(8,128)(2,1)S(1)}, u32[]{:S(2)}, u32[]{:S(2)}) collective-permute-start(bf16[144,256]{1,0:T(8,128)(2,1)} %get-tuple-element.25.refs_0_), channel_id=1, source_target_pairs={{0,4},{1,5},{2,6},{3,7},{4,0},{5,1},{6,2},{7,3},{8,12},{9,13},{10,... | collective-permute-start | bytes 221192 | tf_op jit(solution)/shard_map/ppermute | solution.py:32
  9.9 5.9 %collective-permute-start.2 = (bf16[144,256]{1,0:T(8,128)(2,1)}, bf16[144,256]{1,0:T(8,128)(2,1)S(1)}, u32[]{:S(2)}, u32[]{:S(2)}) collective-permute-start(bf16[144,256]{1,0:T(8,128)(2,1)} %get-tuple-element.17.refs_0_), channel_id=1, source_target_pairs={{0,24},{8,16},{16,8},{24,0},{1,25},{9,17},{17,9},{25,1},{2,26},{10... | collective-permute-start | bytes 221192 | tf_op jit(solution)/shard_map/ppermute | solution.py:32
  9.9 9.3 %collective-permute-start.7 = (bf16[144,256]{1,0:T(8,128)(2,1)}, bf16[144,256]{1,0:T(8,128)(2,1)S(1)}, u32[]{:S(2)}, u32[]{:S(2)}) collective-permute-start(bf16[144,256]{1,0:T(8,128)(2,1)} %get-tuple-element.25.refs_0_), channel_id=1, source_target_pairs={{0,1},{1,0},{2,3},{3,2},{4,5},{5,4},{6,7},{7,6},{8,9},{9,8},{10,11... | collective-permute-start | bytes 221192 | tf_op jit(solution)/shard_map/ppermute | solution.py:332
  11.4 9.1 %collective-permute-start.8 = (bf16[144,256]{1,0:T(8,128)(2,1)}, bf16[144,256]{1,0:T(8,128)(2,1)S(1)}, u32[]{:S(2)}, u32[]{:S(2)}) collective-permute-start(bf16[144,256]{1,0:T(8,128)(2,1)} %get-tuple-element.25.refs_0_), channel_id=1, source_target_pairs={{0,2},{1,3},{2,0},{3,1},{4,6},{5,7},{6,4},{7,5},{8,10},{9,11},{10,... | collective-permute-start | bytes 221192 | tf_op jit(solution)/shard_map/ppermute | solution.py:332
  13.0 9.0 %collective-permute-start.9 = (bf16[144,256]{1,0:T(8,128)(2,1)}, bf16[144,256]{1,0:T(8,128)(2,1)S(1)}, u32[]{:S(2)}, u32[]{:S(2)}) collective-permute-start(bf16[144,256]{1,0:T(8,128)(2,1)} %get-tuple-element.25.refs_0_), channel_id=1, source_target_pairs={{0,3},{1,2},{2,1},{3,0},{4,7},{5,6},{6,5},{7,4},{8,11},{9,10},{10,... | collective-permute-start | bytes 221192 | tf_op jit(solution)/shard_map/ppermute | solution.py:332
  14.4 8.6 %collective-permute-start.11 = (bf16[144,256]{1,0:T(8,128)(2,1)S(1)}, bf16[144,256]{1,0:T(8,128)(2,1)S(1)}, u32[]{:S(2)}, u32[]{:S(2)}) collective-permute-start(bf16[144,256]{1,0:T(8,128)(2,1)S(1)} %collective-permute-done.10.refs_4_), channel_id=1, source_target_pairs={{0,1},{1,0},{2,3},{3,2},{4,5},{5,4},{6,7},{7,6},{8,9},{9,8},{10,11... | collective-permute-start | bytes 221192 | tf_op jit(solution)/shard_map/ppermute | solution.py:332
  15.8 1.2 %copy-start = (bf16[1024,512]{1,0:T(8,128)(2,1)S(1)}, bf16[1024,512]{1,0:T(8,128)(2,1)}, u32[]{:S(2)}) copy-start(bf16[1024,512]{1,0:T(8,128)(2,1)} %get-tuple-element.18.refs_4_.refs_8_) | copy-start | bytes 3145732
  17.0 0.9 %copy-start.2 = (bf16[144,256]{1,0:T(8,128)(2,1)S(1)}, bf16[144,256]{1,0:T(8,128)(2,1)}, u32[]{:S(2)}) copy-start(bf16[144,256]{1,0:T(8,128)(2,1)} %get-tuple-element.17.refs_0_) | copy-start | bytes 221188
  18.5 14.8 %collective-permute-start.3 = (bf16[256,256]{1,0:T(8,128)(2,1)S(1)}, bf16[256,256]{1,0:T(8,128)(2,1)S(1)}, u32[]{:S(2)}, u32[]{:S(2)}) collective-permute-start(bf16[256,256]{1,0:T(8,128)(2,1)S(1)} %get-tuple-element.20), channel_id=1, source_target_pairs={{0,1},{1,0},{2,3},{3,2},{4,5},{5,4},{6,7},{7,6},{8,9},{9,8},{10,11... | collective-permute-start | bytes 393224 | tf_op jit(solution)/shard_map/ppermute | solution.py:332
  19.2 15.3 %collective-permute-start.4 = (bf16[256,256]{1,0:T(8,128)(2,1)S(1)}, bf16[256,256]{1,0:T(8,128)(2,1)S(1)}, u32[]{:S(2)}, u32[]{:S(2)}) collective-permute-start(bf16[256,256]{1,0:T(8,128)(2,1)S(1)} %get-tuple-element.21), channel_id=1, source_target_pairs={{0,2},{1,3},{2,0},{3,1},{4,6},{5,7},{6,4},{7,5},{8,10},{9,11},{10,... | collective-permute-start | bytes 393224 | tf_op jit(solution)/shard_map/ppermute | solution.py:332
  20.5 14.0 %collective-permute-start.5 = (bf16[256,256]{1,0:T(8,128)(2,1)S(1)}, bf16[256,256]{1,0:T(8,128)(2,1)S(1)}, u32[]{:S(2)}, u32[]{:S(2)}) collective-permute-start(bf16[256,256]{1,0:T(8,128)(2,1)S(1)} %get-tuple-element.22), channel_id=1, source_target_pairs={{0,3},{1,2},{2,1},{3,0},{4,7},{5,6},{6,5},{7,4},{8,11},{9,10},{10,... | collective-permute-start | bytes 393224 | tf_op jit(solution)/shard_map/ppermute | solution.py:332
  22.0 7.3 %collective-permute-start.12 = (bf16[144,256]{1,0:T(8,128)(2,1)S(1)}, bf16[144,256]{1,0:T(8,128)(2,1)S(1)}, u32[]{:S(2)}, u32[]{:S(2)}) collective-permute-start(bf16[144,256]{1,0:T(8,128)(2,1)S(1)} %collective-permute-done.10.refs_4_), channel_id=1, source_target_pairs={{0,2},{1,3},{2,0},{3,1},{4,6},{5,7},{6,4},{7,5},{8,10},{9,11},{10,... | collective-permute-start | bytes 221192 | tf_op jit(solution)/shard_map/ppermute | solution.py:332
  22.9 8.0 %collective-permute-start.13 = (bf16[144,256]{1,0:T(8,128)(2,1)S(1)}, bf16[144,256]{1,0:T(8,128)(2,1)S(1)}, u32[]{:S(2)}, u32[]{:S(2)}) collective-permute-start(bf16[144,256]{1,0:T(8,128)(2,1)S(1)} %collective-permute-done.10.refs_4_), channel_id=1, source_target_pairs={{0,3},{1,2},{2,1},{3,0},{4,7},{5,6},{6,5},{7,4},{8,11},{9,10},{10,... | collective-permute-start | bytes 221192 | tf_op jit(solution)/shard_map/ppermute | solution.py:332
  30.9 0.9 %copy-start.1 = (bf16[144,256]{1,0:T(8,128)(2,1)S(1)}, bf16[144,256]{1,0:T(8,128)(2,1)}, u32[]{:S(2)}) copy-start(bf16[144,256]{1,0:T(8,128)(2,1)} %get-tuple-element.25.refs_0_) | copy-start | bytes 221188
  32.5 4.4 %collective-permute-start.14 = (bf16[128,256]{1,0:T(8,128)(2,1)S(1)}, bf16[128,256]{1,0:T(8,128)(2,1)S(1)}, u32[]{:S(2)}, u32[]{:S(2)}) collective-permute-start(bf16[128,256]{1,0:T(8,128)(2,1)S(1)} %get-tuple-element.28), channel_id=1, source_target_pairs={{0,8},{8,0},{16,24},{24,16},{1,9},{9,1},{17,25},{25,17},{2,10},{10... | collective-permute-start | bytes 196616 | tf_op jit(solution)/shard_map/ppermute | solution.py:32
  32.6 5.0 %collective-permute-start.15 = (bf16[128,256]{1,0:T(8,128)(2,1)S(1)}, bf16[128,256]{1,0:T(8,128)(2,1)S(1)}, u32[]{:S(2)}, u32[]{:S(2)}) collective-permute-start(bf16[128,256]{1,0:T(8,128)(2,1)S(1)} %get-tuple-element.29), channel_id=1, source_target_pairs={{0,16},{8,24},{16,0},{24,8},{1,17},{9,25},{17,1},{25,9},{2,18},{10... | collective-permute-start | bytes 196616 | tf_op jit(solution)/shard_map/ppermute | solution.py:32
  33.2 4.7 %collective-permute-start.16 = (bf16[128,256]{1,0:T(8,128)(2,1)S(1)}, bf16[128,256]{1,0:T(8,128)(2,1)S(1)}, u32[]{:S(2)}, u32[]{:S(2)}) collective-permute-start(bf16[128,256]{1,0:T(8,128)(2,1)S(1)} %get-tuple-element.30), channel_id=1, source_target_pairs={{0,24},{8,16},{16,8},{24,0},{1,25},{9,17},{17,9},{25,1},{2,26},{10... | collective-permute-start | bytes 196616 | tf_op jit(solution)/shard_map/ppermute | solution.py:32
  34.5 6.7 %collective-permute-start.6 = (bf16[128,256]{1,0:T(8,128)(2,1)S(1)}, bf16[128,256]{1,0:T(8,128)(2,1)S(1)}, u32[]{:S(2)}, u32[]{:S(2)}) collective-permute-start(bf16[128,256]{1,0:T(8,128)(2,1)S(1)} %get-tuple-element.24), channel_id=1, source_target_pairs={{0,4},{1,5},{2,6},{3,7},{4,0},{5,1},{6,2},{7,3},{8,12},{9,13},{10,... | collective-permute-start | bytes 196616 | tf_op jit(solution)/shard_map/ppermute | solution.py:32

commit v3 on v2

--- a/solution.py
+++ b/solution.py
@@ -297,6 +297,7 @@
     block = tile_len * tile_len
     dense = dst_blocks * slots * block
     rows_in = (slots + 2 * dst_blocks) * tile_len * width
+    PLACE = 2 * tile_count * block + 6 * dense + 8 * rows_in
     FORWARD = 3 * dense + 8 * rows_in
     BACKWARD = 3 * dense + 8 * rows_in
     FINISH = 4 * rows_in
@@ -318,9 +319,14 @@
             pltpu.SMEM((tile_count + 1,), jnp.int32),
             pltpu.SemaphoreType.DMA((chunks + 3,)),
         ],
-        compiler_params=room(60 * 1024 * 1024),
+        compiler_params=room(PLACE),
         name="place",
-    )(jnp.transpose(tile_list, (1, 0, 2)), features, grad_out, tile_weight)
+    )(
+        *(
+            pltpu.with_memory_space_constraint(operand, pltpu.HBM)
+            for operand in (jnp.transpose(tile_list, (1, 0, 2)), features, grad_out, tile_weight)
+        )
+    )
 
     own_rows = grad_out.shape[0]
     halves = 2 if col_count >= 4 and col_count & (col_count - 1) == 0 else 1

time: 42.2 us -> 37.9 us (0.90)
  local copies, waits for them, and re-layouts: 2.99 us -> 0 us
  Pallas kernels: 6.2 us -> 5.18 us
    unnamed x6 -> x0, local copies, waits for them, and re-layouts: 2.99 us -> none
    pallas_call x1, Pallas kernels: 3.53 us -> 2.49 us  [aggregate(): pl.pallas_call(functools.partial(place_kernel, chunks, src_blocks), out_s...]
where the time goes in v3:
time: 37.9 us; the launch traced here: 37.7 us
  starting transfers between devices  20.5 us (54%)
  waiting for transfers between devices  11.2 us (30%)
  Pallas kernels  5.18 us (14%)
  between operations  0.68 us (2%)
    ppermute x9, starting transfers between devices, near(): return lax.ppermute(value, 'col', [(c, c ^ k) for c in range(col_count)])  10.5 us
    ppermute x8, starting transfers between devices, exchange(): return lax.ppermute(value, axis, pairs)  10 us
    ppermute x9, waiting for transfers between devices, near(): return lax.ppermute(value, 'col', [(c, c ^ k) for c in range(col_count)])  6.82 us
    ppermute x8, waiting for transfers between devices, exchange(): return lax.ppermute(value, axis, pairs)  4.42 us
    pallas_call x1, Pallas kernels, aggregate(): pl.pallas_call(functools.partial(place_kernel, chunks, src_blocks), out_s...  2.49 us
    pallas_call x2, Pallas kernels, finish(): pl.pallas_call(finish_kernel, out_shape=shape((rows, width), BF16), in_sp...  1.32 us
  transfers between devices with their start and end apart: 17, of which 6 were waited for; matrix products, arithmetic and copies ran while one was open for 0% of the time, Pallas kernels for 5%

profile of v3, /device:TPU:0, one launch (start us, length us, event | category | flops | bytes accessed | tf_op | source)
XLA Modules:
  0.0 37.7 jit_solution(2818193464409015109)
XLA Ops:
  0.6 2.5 %place.1 = (bf16[1024,512]{1,0:T(8,128)(2,1)S(1)}, bf16[144,256]{1,0:T(8,128)(2,1)S(1)}, bf16[144,256]{1,0:T(8,128)(2,1)S(1)}) custom-call(s32[3,4,32]{2,1,0:T(4,128)} %bitcast.1, bf16[128,256]{1,0:T(8,128)(2,1)} %features_hbm.1, bf16[128,256]{1,0:T(8,128)(2,1)} %grads_hbm.1, bf16[64,128,128]{2,1,0:T(8,128)(2,1)} %tiles_hbm.1), custom_call_target="tpu_custom_call" | custom-call | tf_op jit(solution)/shard_map/place/pallas_call | solution.py:305
  3.1 0.5 %collective-permute-start = (bf16[144,256]{1,0:T(8,128)(2,1)S(1)}, bf16[144,256]{1,0:T(8,128)(2,1)S(1)}, u32[]{:S(2)}, u32[]{:S(2)}) collective-permute-start(bf16[144,256]{1,0:T(8,128)(2,1)S(1)} %get-tuple-element.17.refs_0_), channel_id=1, source_target_pairs={{0,8},{8,0},{16,24},{24,16},{1,9},{9,1},{17,25},{25,17},{2,10},{10... | collective-permute-start | bytes 221192 | tf_op jit(solution)/shard_map/ppermute | solution.py:32
  3.7 2.6 %collective-permute-start.1 = (bf16[144,256]{1,0:T(8,128)(2,1)S(1)}, bf16[144,256]{1,0:T(8,128)(2,1)S(1)}, u32[]{:S(2)}, u32[]{:S(2)}) collective-permute-start(bf16[144,256]{1,0:T(8,128)(2,1)S(1)} %get-tuple-element.17.refs_0_), channel_id=1, source_target_pairs={{0,16},{8,24},{16,0},{24,8},{1,17},{9,25},{17,1},{25,9},{2,18},{10... | collective-permute-start | bytes 221192 | tf_op jit(solution)/shard_map/ppermute | solution.py:32
  6.3 2.6 %collective-permute-start.10 = (bf16[144,256]{1,0:T(8,128)(2,1)S(1)}, bf16[144,256]{1,0:T(8,128)(2,1)S(1)}, u32[]{:S(2)}, u32[]{:S(2)}) collective-permute-start(bf16[144,256]{1,0:T(8,128)(2,1)S(1)} %get-tuple-element.25.refs_0_), channel_id=1, source_target_pairs={{0,4},{1,5},{2,6},{3,7},{4,0},{5,1},{6,2},{7,3},{8,12},{9,13},{10,... | collective-permute-start | bytes 221192 | tf_op jit(solution)/shard_map/ppermute | solution.py:32
  8.8 0.0 collective-permute-start.2
  8.8 1.5 %collective-permute-start.7 = (bf16[144,256]{1,0:T(8,128)(2,1)S(1)}, bf16[144,256]{1,0:T(8,128)(2,1)S(1)}, u32[]{:S(2)}, u32[]{:S(2)}) collective-permute-start(bf16[144,256]{1,0:T(8,128)(2,1)S(1)} %get-tuple-element.25.refs_0_), channel_id=1, source_target_pairs={{0,1},{1,0},{2,3},{3,2},{4,5},{5,4},{6,7},{7,6},{8,9},{9,8},{10,11... | collective-permute-start | bytes 221192 | tf_op jit(solution)/shard_map/ppermute | solution.py:338
  10.4 0.0 collective-permute-done.refs_1_
  10.4 1.6 %collective-permute-start.8 = (bf16[144,256]{1,0:T(8,128)(2,1)S(1)}, bf16[144,256]{1,0:T(8,128)(2,1)S(1)}, u32[]{:S(2)}, u32[]{:S(2)}) collective-permute-start(bf16[144,256]{1,0:T(8,128)(2,1)S(1)} %get-tuple-element.25.refs_0_), channel_id=1, source_target_pairs={{0,2},{1,3},{2,0},{3,1},{4,6},{5,7},{6,4},{7,5},{8,10},{9,11},{10,... | collective-permute-start | bytes 221192 | tf_op jit(solution)/shard_map/ppermute | solution.py:338
  11.9 0.0 collective-permute-done.1.refs_2_
  11.9 0.4 %collective-permute-start.9 = (bf16[144,256]{1,0:T(8,128)(2,1)S(1)}, bf16[144,256]{1,0:T(8,128)(2,1)S(1)}, u32[]{:S(2)}, u32[]{:S(2)}) collective-permute-start(bf16[144,256]{1,0:T(8,128)(2,1)S(1)} %get-tuple-element.25.refs_0_), channel_id=1, source_target_pairs={{0,3},{1,2},{2,1},{3,0},{4,7},{5,6},{6,5},{7,4},{8,11},{9,10},{10,... | collective-permute-start | bytes 221192 | tf_op jit(solution)/shard_map/ppermute | solution.py:338
  12.3 0.8 %collective-permute-done.10.refs_4_ = bf16[144,256]{1,0:T(8,128)(2,1)S(1)} collective-permute-done((bf16[144,256]{1,0:T(8,128)(2,1)S(1)}, bf16[144,256]{1,0:T(8,128)(2,1)S(1)}, u32[]{:S(2)}, u32[]{:S(2)}) %collective-permute-start.10) | collective-permute-done | bytes 73760 | tf_op jit(solution)/shard_map/ppermute | solution.py:32
  13.1 1.4 %collective-permute-start.11 = (bf16[144,256]{1,0:T(8,128)(2,1)S(1)}, bf16[144,256]{1,0:T(8,128)(2,1)S(1)}, u32[]{:S(2)}, u32[]{:S(2)}) collective-permute-start(bf16[144,256]{1,0:T(8,128)(2,1)S(1)} %collective-permute-done.10.refs_4_), channel_id=1, source_target_pairs={{0,1},{1,0},{2,3},{3,2},{4,5},{5,4},{6,7},{7,6},{8,9},{9,8},{10,11... | collective-permute-start | bytes 221192 | tf_op jit(solution)/shard_map/ppermute | solution.py:338
  14.5 0.0 collective-permute-done.2.refs_3_
  14.5 0.6 %forward.1 = (f32[256,256]{1,0:T(8,128)S(1)}, bf16[256,256]{1,0:T(8,128)(2,1)S(1)}, bf16[256,256]{1,0:T(8,128)(2,1)S(1)}, bf16[256,256]{1,0:T(8,128)(2,1)S(1)}, f32[128,128]{1,0:T(8,128)S(1)}) custom-call(bf16[144,256]{1,0:T(8,128)(2,1)S(1)} %get-tuple-element.17.refs_0_, bf16[144,256]{1,0:T(8,128)(2,1)S(1)} %collective-permute-done.refs_1_, ...), custom_call_target="tpu_custom_call" | custom-call | tf_op jit(solution)/shard_map/forward/pallas_call | solution.py:347
  15.1 0.7 %collective-permute-start.3 = (bf16[256,256]{1,0:T(8,128)(2,1)S(1)}, bf16[256,256]{1,0:T(8,128)(2,1)S(1)}, u32[]{:S(2)}, u32[]{:S(2)}) collective-permute-start(bf16[256,256]{1,0:T(8,128)(2,1)S(1)} %get-tuple-element.20), channel_id=1, source_target_pairs={{0,1},{1,0},{2,3},{3,2},{4,5},{5,4},{6,7},{7,6},{8,9},{9,8},{10,11... | collective-permute-start | bytes 393224 | tf_op jit(solution)/shard_map/ppermute | solution.py:338
  15.8 0.0 collective-permute-done.7.refs_1_
  15.8 1.3 %collective-permute-start.4 = (bf16[256,256]{1,0:T(8,128)(2,1)S(1)}, bf16[256,256]{1,0:T(8,128)(2,1)S(1)}, u32[]{:S(2)}, u32[]{:S(2)}) collective-permute-start(bf16[256,256]{1,0:T(8,128)(2,1)S(1)} %get-tuple-element.21), channel_id=1, source_target_pairs={{0,2},{1,3},{2,0},{3,1},{4,6},{5,7},{6,4},{7,5},{8,10},{9,11},{10,... | collective-permute-start | bytes 393224 | tf_op jit(solution)/shard_map/ppermute | solution.py:338
  17.1 0.0 collective-permute-done.8.refs_2_
  17.1 1.5 %collective-permute-start.5 = (bf16[256,256]{1,0:T(8,128)(2,1)S(1)}, bf16[256,256]{1,0:T(8,128)(2,1)S(1)}, u32[]{:S(2)}, u32[]{:S(2)}) collective-permute-start(bf16[256,256]{1,0:T(8,128)(2,1)S(1)} %get-tuple-element.22), channel_id=1, source_target_pairs={{0,3},{1,2},{2,1},{3,0},{4,7},{5,6},{6,5},{7,4},{8,11},{9,10},{10,... | collective-permute-start | bytes 393224 | tf_op jit(solution)/shard_map/ppermute | solution.py:338
  18.7 0.0 collective-permute-done.9.refs_3_
  18.7 0.9 %collective-permute-start.12 = (bf16[144,256]{1,0:T(8,128)(2,1)S(1)}, bf16[144,256]{1,0:T(8,128)(2,1)S(1)}, u32[]{:S(2)}, u32[]{:S(2)}) collective-permute-start(bf16[144,256]{1,0:T(8,128)(2,1)S(1)} %collective-permute-done.10.refs_4_), channel_id=1, source_target_pairs={{0,2},{1,3},{2,0},{3,1},{4,6},{5,7},{6,4},{7,5},{8,10},{9,11},{10,... | collective-permute-start | bytes 221192 | tf_op jit(solution)/shard_map/ppermute | solution.py:338
  19.6 0.0 collective-permute-done.11.refs_5_
  19.6 1.2 %collective-permute-start.13 = (bf16[144,256]{1,0:T(8,128)(2,1)S(1)}, bf16[144,256]{1,0:T(8,128)(2,1)S(1)}, u32[]{:S(2)}, u32[]{:S(2)}) collective-permute-start(bf16[144,256]{1,0:T(8,128)(2,1)S(1)} %collective-permute-done.10.refs_4_), channel_id=1, source_target_pairs={{0,3},{1,2},{2,1},{3,0},{4,7},{5,6},{6,5},{7,4},{8,11},{9,10},{10,... | collective-permute-start | bytes 221192 | tf_op jit(solution)/shard_map/ppermute | solution.py:338
  20.8 5.2 %collective-permute-done.12.refs_6_ = bf16[144,256]{1,0:T(8,128)(2,1)S(1)} collective-permute-done((bf16[144,256]{1,0:T(8,128)(2,1)S(1)}, bf16[144,256]{1,0:T(8,128)(2,1)S(1)}, u32[]{:S(2)}, u32[]{:S(2)}) %collective-permute-start.12) | collective-permute-done | bytes 73760 | tf_op jit(solution)/shard_map/ppermute | solution.py:338
  26.0 1.6 %collective-permute-done.13.refs_7_ = bf16[144,256]{1,0:T(8,128)(2,1)S(1)} collective-permute-done((bf16[144,256]{1,0:T(8,128)(2,1)S(1)}, bf16[144,256]{1,0:T(8,128)(2,1)S(1)}, u32[]{:S(2)}, u32[]{:S(2)}) %collective-permute-start.13) | collective-permute-done | bytes 73760 | tf_op jit(solution)/shard_map/ppermute | solution.py:338
  27.6 0.7 %backward.1 = (f32[128,256]{1,0:T(8,128)S(1)}, bf16[128,256]{1,0:T(8,128)(2,1)S(1)}, bf16[128,256]{1,0:T(8,128)(2,1)S(1)}, bf16[128,256]{1,0:T(8,128)(2,1)S(1)}, f32[128,128]{1,0:T(8,128)S(1)}) custom-call(bf16[144,256]{1,0:T(8,128)(2,1)S(1)} %get-tuple-element.25.refs_0_, bf16[144,256]{1,0:T(8,128)(2,1)S(1)} %collective-permute-done.7.refs_1_, ...), custom_call_target="tpu_custom_call" | custom-call | tf_op jit(solution)/shard_map/backward/pallas_call | solution.py:373
  28.3 0.1 collective-permute-start.14
  28.4 0.6 %collective-permute-start.15 = (bf16[128,256]{1,0:T(8,128)(2,1)S(1)}, bf16[128,256]{1,0:T(8,128)(2,1)S(1)}, u32[]{:S(2)}, u32[]{:S(2)}) collective-permute-start(bf16[128,256]{1,0:T(8,128)(2,1)S(1)} %get-tuple-element.29), channel_id=1, source_target_pairs={{0,16},{8,24},{16,0},{24,8},{1,17},{9,25},{17,1},{25,9},{2,18},{10... | collective-permute-start | bytes 196616 | tf_op jit(solution)/shard_map/ppermute | solution.py:32
  29.0 0.0 collective-permute-done.3.refs_1_
  29.0 1.2 %collective-permute-start.16 = (bf16[128,256]{1,0:T(8,128)(2,1)S(1)}, bf16[128,256]{1,0:T(8,128)(2,1)S(1)}, u32[]{:S(2)}, u32[]{:S(2)}) collective-permute-start(bf16[128,256]{1,0:T(8,128)(2,1)S(1)} %get-tuple-element.30), channel_id=1, source_target_pairs={{0,24},{8,16},{16,8},{24,0},{1,25},{9,17},{17,9},{25,1},{2,26},{10... | collective-permute-start | bytes 196616 | tf_op jit(solution)/shard_map/ppermute | solution.py:32
  30.2 0.0 collective-permute-done.4.refs_2_
  30.2 0.0 collective-permute-done.5.refs_3_
  30.2 0.1 merge.1
  30.3 2.4 %collective-permute-start.6 = (bf16[128,256]{1,0:T(8,128)(2,1)S(1)}, bf16[128,256]{1,0:T(8,128)(2,1)S(1)}, u32[]{:S(2)}, u32[]{:S(2)}) collective-permute-start(bf16[128,256]{1,0:T(8,128)(2,1)S(1)} %get-tuple-element.24), channel_id=1, source_target_pairs={{0,4},{1,5},{2,6},{3,7},{4,0},{5,1},{6,2},{7,3},{8,12},{9,13},{10,... | collective-permute-start | bytes 196616 | tf_op jit(solution)/shard_map/ppermute | solution.py:32
  32.7 0.0 collective-permute-done.14.refs_1_
  32.7 0.7 %collective-permute-done.15.refs_2_ = bf16[128,256]{1,0:T(8,128)(2,1)S(1)} collective-permute-done((bf16[128,256]{1,0:T(8,128)(2,1)S(1)}, bf16[128,256]{1,0:T(8,128)(2,1)S(1)}, u32[]{:S(2)}, u32[]{:S(2)}) %collective-permute-start.15) | collective-permute-done | bytes 65568 | tf_op jit(solution)/shard_map/ppermute | solution.py:32
  33.4 0.3 collective-permute-done.16.refs_3_
  33.7 0.7 %finish.3 = bf16[128,256]{1,0:T(8,128)(2,1)} custom-call(f32[128,256]{1,0:T(8,128)S(1)} %get-tuple-element.27.refs_0_, bf16[128,256]{1,0:T(8,128)(2,1)S(1)} %collective-permute-done.14.refs_1_, bf16[128,256]{1,0:T(8,128)(2,1)S(1)} %collective-permute-done.15.refs_2_, bf16[128,256]{1,0:T(8,128)(2,1)S(1)} %collective-permute-done.16.refs_3_, ...), custom_call_target="tpu_custom_call" | custom-call | tf_op jit(solution)/shard_map/finish/pallas_call | solution.py:396
  34.4 2.6 %collective-permute-done.6.refs_1_ = bf16[128,256]{1,0:T(8,128)(2,1)S(1)} collective-permute-done((bf16[128,256]{1,0:T(8,128)(2,1)S(1)}, bf16[128,256]{1,0:T(8,128)(2,1)S(1)}, u32[]{:S(2)}, u32[]{:S(2)}) %collective-permute-start.6) | collective-permute-done | bytes 65568 | tf_op jit(solution)/shard_map/ppermute | solution.py:32
  37.0 0.7 %finish.2 = bf16[128,256]{1,0:T(8,128)(2,1)} custom-call(f32[128,256]{1,0:T(8,128)S(1)} %get-tuple-element.23.refs_0_, bf16[128,256]{1,0:T(8,128)(2,1)S(1)} %collective-permute-done.6.refs_1_, f32[128,128]{1,0:T(8,128)S(1)} %get-tuple-element.26.refs_2_), custom_call_target="tpu_custom_call" | custom-call | tf_op jit(solution)/shard_map/finish/pallas_call | solution.py:396
Async XLA Ops:
  3.1 7.2 %collective-permute-start = (bf16[144,256]{1,0:T(8,128)(2,1)S(1)}, bf16[144,256]{1,0:T(8,128)(2,1)S(1)}, u32[]{:S(2)}, u32[]{:S(2)}) collective-permute-start(bf16[144,256]{1,0:T(8,128)(2,1)S(1)} %get-tuple-element.17.refs_0_), channel_id=1, source_target_pairs={{0,8},{8,0},{16,24},{24,16},{1,9},{9,1},{17,25},{25,17},{2,10},{10... | collective-permute-start | bytes 221192 | tf_op jit(solution)/shard_map/ppermute | solution.py:32
  3.7 8.3 %collective-permute-start.1 = (bf16[144,256]{1,0:T(8,128)(2,1)S(1)}, bf16[144,256]{1,0:T(8,128)(2,1)S(1)}, u32[]{:S(2)}, u32[]{:S(2)}) collective-permute-start(bf16[144,256]{1,0:T(8,128)(2,1)S(1)} %get-tuple-element.17.refs_0_), channel_id=1, source_target_pairs={{0,16},{8,24},{16,0},{24,8},{1,17},{9,25},{17,1},{25,9},{2,18},{10... | collective-permute-start | bytes 221192 | tf_op jit(solution)/shard_map/ppermute | solution.py:32
  6.3 6.8 %collective-permute-start.10 = (bf16[144,256]{1,0:T(8,128)(2,1)S(1)}, bf16[144,256]{1,0:T(8,128)(2,1)S(1)}, u32[]{:S(2)}, u32[]{:S(2)}) collective-permute-start(bf16[144,256]{1,0:T(8,128)(2,1)S(1)} %get-tuple-element.25.refs_0_), channel_id=1, source_target_pairs={{0,4},{1,5},{2,6},{3,7},{4,0},{5,1},{6,2},{7,3},{8,12},{9,13},{10,... | collective-permute-start | bytes 221192 | tf_op jit(solution)/shard_map/ppermute | solution.py:32
  8.8 5.7 %collective-permute-start.2 = (bf16[144,256]{1,0:T(8,128)(2,1)S(1)}, bf16[144,256]{1,0:T(8,128)(2,1)S(1)}, u32[]{:S(2)}, u32[]{:S(2)}) collective-permute-start(bf16[144,256]{1,0:T(8,128)(2,1)S(1)} %get-tuple-element.17.refs_0_), channel_id=1, source_target_pairs={{0,24},{8,16},{16,8},{24,0},{1,25},{9,17},{17,9},{25,1},{2,26},{10... | collective-permute-start | bytes 221192 | tf_op jit(solution)/shard_map/ppermute | solution.py:32
  8.8 7.0 %collective-permute-start.7 = (bf16[144,256]{1,0:T(8,128)(2,1)S(1)}, bf16[144,256]{1,0:T(8,128)(2,1)S(1)}, u32[]{:S(2)}, u32[]{:S(2)}) collective-permute-start(bf16[144,256]{1,0:T(8,128)(2,1)S(1)} %get-tuple-element.25.refs_0_), channel_id=1, source_target_pairs={{0,1},{1,0},{2,3},{3,2},{4,5},{5,4},{6,7},{7,6},{8,9},{9,8},{10,11... | collective-permute-start | bytes 221192 | tf_op jit(solution)/shard_map/ppermute | solution.py:338
  10.4 6.8 %collective-permute-start.8 = (bf16[144,256]{1,0:T(8,128)(2,1)S(1)}, bf16[144,256]{1,0:T(8,128)(2,1)S(1)}, u32[]{:S(2)}, u32[]{:S(2)}) collective-permute-start(bf16[144,256]{1,0:T(8,128)(2,1)S(1)} %get-tuple-element.25.refs_0_), channel_id=1, source_target_pairs={{0,2},{1,3},{2,0},{3,1},{4,6},{5,7},{6,4},{7,5},{8,10},{9,11},{10,... | collective-permute-start | bytes 221192 | tf_op jit(solution)/shard_map/ppermute | solution.py:338
  11.9 6.7 %collective-permute-start.9 = (bf16[144,256]{1,0:T(8,128)(2,1)S(1)}, bf16[144,256]{1,0:T(8,128)(2,1)S(1)}, u32[]{:S(2)}, u32[]{:S(2)}) collective-permute-start(bf16[144,256]{1,0:T(8,128)(2,1)S(1)} %get-tuple-element.25.refs_0_), channel_id=1, source_target_pairs={{0,3},{1,2},{2,1},{3,0},{4,7},{5,6},{6,5},{7,4},{8,11},{9,10},{10,... | collective-permute-start | bytes 221192 | tf_op jit(solution)/shard_map/ppermute | solution.py:338
  13.1 6.5 %collective-permute-start.11 = (bf16[144,256]{1,0:T(8,128)(2,1)S(1)}, bf16[144,256]{1,0:T(8,128)(2,1)S(1)}, u32[]{:S(2)}, u32[]{:S(2)}) collective-permute-start(bf16[144,256]{1,0:T(8,128)(2,1)S(1)} %collective-permute-done.10.refs_4_), channel_id=1, source_target_pairs={{0,1},{1,0},{2,3},{3,2},{4,5},{5,4},{6,7},{7,6},{8,9},{9,8},{10,11... | collective-permute-start | bytes 221192 | tf_op jit(solution)/shard_map/ppermute | solution.py:338
  15.1 13.9 %collective-permute-start.3 = (bf16[256,256]{1,0:T(8,128)(2,1)S(1)}, bf16[256,256]{1,0:T(8,128)(2,1)S(1)}, u32[]{:S(2)}, u32[]{:S(2)}) collective-permute-start(bf16[256,256]{1,0:T(8,128)(2,1)S(1)} %get-tuple-element.20), channel_id=1, source_target_pairs={{0,1},{1,0},{2,3},{3,2},{4,5},{5,4},{6,7},{7,6},{8,9},{9,8},{10,11... | collective-permute-start | bytes 393224 | tf_op jit(solution)/shard_map/ppermute | solution.py:338
  15.8 14.4 %collective-permute-start.4 = (bf16[256,256]{1,0:T(8,128)(2,1)S(1)}, bf16[256,256]{1,0:T(8,128)(2,1)S(1)}, u32[]{:S(2)}, u32[]{:S(2)}) collective-permute-start(bf16[256,256]{1,0:T(8,128)(2,1)S(1)} %get-tuple-element.21), channel_id=1, source_target_pairs={{0,2},{1,3},{2,0},{3,1},{4,6},{5,7},{6,4},{7,5},{8,10},{9,11},{10,... | collective-permute-start | bytes 393224 | tf_op jit(solution)/shard_map/ppermute | solution.py:338
  17.1 13.1 %collective-permute-start.5 = (bf16[256,256]{1,0:T(8,128)(2,1)S(1)}, bf16[256,256]{1,0:T(8,128)(2,1)S(1)}, u32[]{:S(2)}, u32[]{:S(2)}) collective-permute-start(bf16[256,256]{1,0:T(8,128)(2,1)S(1)} %get-tuple-element.22), channel_id=1, source_target_pairs={{0,3},{1,2},{2,1},{3,0},{4,7},{5,6},{6,5},{7,4},{8,11},{9,10},{10,... | collective-permute-start | bytes 393224 | tf_op jit(solution)/shard_map/ppermute | solution.py:338
  18.7 7.3 %collective-permute-start.12 = (bf16[144,256]{1,0:T(8,128)(2,1)S(1)}, bf16[144,256]{1,0:T(8,128)(2,1)S(1)}, u32[]{:S(2)}, u32[]{:S(2)}) collective-permute-start(bf16[144,256]{1,0:T(8,128)(2,1)S(1)} %collective-permute-done.10.refs_4_), channel_id=1, source_target_pairs={{0,2},{1,3},{2,0},{3,1},{4,6},{5,7},{6,4},{7,5},{8,10},{9,11},{10,... | collective-permute-start | bytes 221192 | tf_op jit(solution)/shard_map/ppermute | solution.py:338
  19.6 8.0 %collective-permute-start.13 = (bf16[144,256]{1,0:T(8,128)(2,1)S(1)}, bf16[144,256]{1,0:T(8,128)(2,1)S(1)}, u32[]{:S(2)}, u32[]{:S(2)}) collective-permute-start(bf16[144,256]{1,0:T(8,128)(2,1)S(1)} %collective-permute-done.10.refs_4_), channel_id=1, source_target_pairs={{0,3},{1,2},{2,1},{3,0},{4,7},{5,6},{6,5},{7,4},{8,11},{9,10},{10,... | collective-permute-start | bytes 221192 | tf_op jit(solution)/shard_map/ppermute | solution.py:338
  28.3 4.4 %collective-permute-start.14 = (bf16[128,256]{1,0:T(8,128)(2,1)S(1)}, bf16[128,256]{1,0:T(8,128)(2,1)S(1)}, u32[]{:S(2)}, u32[]{:S(2)}) collective-permute-start(bf16[128,256]{1,0:T(8,128)(2,1)S(1)} %get-tuple-element.28), channel_id=1, source_target_pairs={{0,8},{8,0},{16,24},{24,16},{1,9},{9,1},{17,25},{25,17},{2,10},{10... | collective-permute-start | bytes 196616 | tf_op jit(solution)/shard_map/ppermute | solution.py:32
  28.4 5.0 %collective-permute-start.15 = (bf16[128,256]{1,0:T(8,128)(2,1)S(1)}, bf16[128,256]{1,0:T(8,128)(2,1)S(1)}, u32[]{:S(2)}, u32[]{:S(2)}) collective-permute-start(bf16[128,256]{1,0:T(8,128)(2,1)S(1)} %get-tuple-element.29), channel_id=1, source_target_pairs={{0,16},{8,24},{16,0},{24,8},{1,17},{9,25},{17,1},{25,9},{2,18},{10... | collective-permute-start | bytes 196616 | tf_op jit(solution)/shard_map/ppermute | solution.py:32
  29.0 4.7 %collective-permute-start.16 = (bf16[128,256]{1,0:T(8,128)(2,1)S(1)}, bf16[128,256]{1,0:T(8,128)(2,1)S(1)}, u32[]{:S(2)}, u32[]{:S(2)}) collective-permute-start(bf16[128,256]{1,0:T(8,128)(2,1)S(1)} %get-tuple-element.30), channel_id=1, source_target_pairs={{0,24},{8,16},{16,8},{24,0},{1,25},{9,17},{17,9},{25,1},{2,26},{10... | collective-permute-start | bytes 196616 | tf_op jit(solution)/shard_map/ppermute | solution.py:32
  30.3 6.7 %collective-permute-start.6 = (bf16[128,256]{1,0:T(8,128)(2,1)S(1)}, bf16[128,256]{1,0:T(8,128)(2,1)S(1)}, u32[]{:S(2)}, u32[]{:S(2)}) collective-permute-start(bf16[128,256]{1,0:T(8,128)(2,1)S(1)} %get-tuple-element.24), channel_id=1, source_target_pairs={{0,4},{1,5},{2,6},{3,7},{4,0},{5,1},{6,2},{7,3},{8,12},{9,13},{10,... | collective-permute-start | bytes 196616 | tf_op jit(solution)/shard_map/ppermute | solution.py:32

commit v4 on v3

--- a/solution.py
+++ b/solution.py
@@ -135,11 +135,11 @@
     for copy in row_copies:
         copy.start()
 
-    @pl.loop(0, pairs + 1)
+    @pl.loop(0, pairs + 1, unroll=3 if (pairs + 1) % 3 == 0 else 1)
     def _(p):
         total_ref[p] = jnp.zeros((tile_len, tile_len), F32)
 
-    @pl.loop(0, tile_count, unroll=8 if tile_count % 8 == 0 else 1)
+    @pl.loop(0, tile_count, unroll=32 if tile_count % 32 == 0 else 1)
     def _(t):
         where_ref[t] = pairs
 
@@ -148,7 +148,7 @@
     for step in range(step_count):
         first = lax.rem(row_pos - step + step_count, step_count) * src_blocks
 
-        @pl.loop(0, slot_count, unroll=8 if slot_count % 8 == 0 else 1)
+        @pl.loop(0, slot_count, unroll=32 if slot_count % 32 == 0 else 1)
         def _(k):
             t = list_ref[0, step, k]
             pair = list_ref[2, step, k] * slots + first + list_ref[1, step, k]
@@ -157,7 +157,7 @@
     for i in range(chunks):
         chunk_copy(i).wait()
 
-        @pl.loop(i * per_chunk, (i + 1) * per_chunk, unroll=4 if per_chunk % 4 == 0 else 1)
+        @pl.loop(i * per_chunk, (i + 1) * per_chunk, unroll=8 if per_chunk % 8 == 0 else 1)
         def _(t):
             p = where_ref[t]
             total_ref[p] = total_ref[p] + tiles_ref[t].astype(F32)
@@ -337,7 +337,10 @@
             return exchange(value, "col", k)
         return lax.ppermute(value, "col", [(c, c ^ k) for c in range(col_count)])
 
-    src_messages = [src_send] + [exchange(src_send, "row", k) for k in range(1, row_count)]
+    def row(value, k):
+        return exchange(value, "row", k)
+
+    src_messages = [src_send] + [row(src_send, k) for k in range(1, row_count)]
     if halves == 2:
         far_send = exchange(dst_send, "col", group)
     dst_messages = [dst_send] + [near(dst_send, k) for k in range(1, group)]
@@ -389,7 +392,7 @@
         name="backward",
     )(*dst_messages, adjacency)
     src_partials = back_partials[:1] + [
-        exchange(back_partials[k], "row", k) for k in range(1, row_count)
+        row(back_partials[k], k) for k in range(1, row_count)
     ]
 
     def finish(received, scale, rows):

time: 37.9 us -> 37.5 us (0.989)
  no operation moved by 1% of the time
where the time goes in v4:
time: 37.5 us; the launch traced here: 37.3 us
  starting transfers between devices  20.6 us (55%)
  waiting for transfers between devices  11.3 us (30%)
  Pallas kernels  4.84 us (13%)
  between operations  0.68 us (2%)
    ppermute x9, starting transfers between devices, near(): return lax.ppermute(value, 'col', [(c, c ^ k) for c in range(col_count)])  10.5 us
    ppermute x8, starting transfers between devices, exchange(): return lax.ppermute(value, axis, pairs)  10 us
    ppermute x9, waiting for transfers between devices, near(): return lax.ppermute(value, 'col', [(c, c ^ k) for c in range(col_count)])  6.84 us
    ppermute x8, waiting for transfers between devices, exchange(): return lax.ppermute(value, axis, pairs)  4.41 us
    pallas_call x1, Pallas kernels, aggregate(): pl.pallas_call(functools.partial(place_kernel, chunks, src_blocks), out_s...  2.17 us
    pallas_call x2, Pallas kernels, finish(): pl.pallas_call(finish_kernel, out_shape=shape((rows, width), BF16), in_sp...  1.32 us
  transfers between devices with their start and end apart: 17, of which 6 were waited for; matrix products, arithmetic and copies ran while one was open for 0% of the time, Pallas kernels for 5%

profile of v4, /device:TPU:0, one launch (start us, length us, event | category | flops | bytes accessed | tf_op | source)
XLA Modules:
  0.0 37.3 jit_solution(13066296501916877639)
XLA Ops:
  0.6 2.2 %place.1 = (bf16[1024,512]{1,0:T(8,128)(2,1)S(1)}, bf16[144,256]{1,0:T(8,128)(2,1)S(1)}, bf16[144,256]{1,0:T(8,128)(2,1)S(1)}) custom-call(s32[3,4,32]{2,1,0:T(4,128)} %bitcast.1, bf16[128,256]{1,0:T(8,128)(2,1)} %features_hbm.1, bf16[128,256]{1,0:T(8,128)(2,1)} %grads_hbm.1, bf16[64,128,128]{2,1,0:T(8,128)(2,1)} %tiles_hbm.1), custom_call_target="tpu_custom_call" | custom-call | tf_op jit(solution)/shard_map/place/pallas_call | solution.py:305
  2.8 0.6 %collective-permute-start = (bf16[144,256]{1,0:T(8,128)(2,1)S(1)}, bf16[144,256]{1,0:T(8,128)(2,1)S(1)}, u32[]{:S(2)}, u32[]{:S(2)}) collective-permute-start(bf16[144,256]{1,0:T(8,128)(2,1)S(1)} %get-tuple-element.17.refs_0_), channel_id=1, source_target_pairs={{0,8},{8,0},{16,24},{24,16},{1,9},{9,1},{17,25},{25,17},{2,10},{10... | collective-permute-start | bytes 221192 | tf_op jit(solution)/shard_map/ppermute | solution.py:32
  3.4 2.6 %collective-permute-start.1 = (bf16[144,256]{1,0:T(8,128)(2,1)S(1)}, bf16[144,256]{1,0:T(8,128)(2,1)S(1)}, u32[]{:S(2)}, u32[]{:S(2)}) collective-permute-start(bf16[144,256]{1,0:T(8,128)(2,1)S(1)} %get-tuple-element.17.refs_0_), channel_id=1, source_target_pairs={{0,16},{8,24},{16,0},{24,8},{1,17},{9,25},{17,1},{25,9},{2,18},{10... | collective-permute-start | bytes 221192 | tf_op jit(solution)/shard_map/ppermute | solution.py:32
  5.9 2.6 %collective-permute-start.10 = (bf16[144,256]{1,0:T(8,128)(2,1)S(1)}, bf16[144,256]{1,0:T(8,128)(2,1)S(1)}, u32[]{:S(2)}, u32[]{:S(2)}) collective-permute-start(bf16[144,256]{1,0:T(8,128)(2,1)S(1)} %get-tuple-element.25.refs_0_), channel_id=1, source_target_pairs={{0,4},{1,5},{2,6},{3,7},{4,0},{5,1},{6,2},{7,3},{8,12},{9,13},{10,... | collective-permute-start | bytes 221192 | tf_op jit(solution)/shard_map/ppermute | solution.py:32
  8.5 0.0 collective-permute-start.2
  8.5 1.5 %collective-permute-start.7 = (bf16[144,256]{1,0:T(8,128)(2,1)S(1)}, bf16[144,256]{1,0:T(8,128)(2,1)S(1)}, u32[]{:S(2)}, u32[]{:S(2)}) collective-permute-start(bf16[144,256]{1,0:T(8,128)(2,1)S(1)} %get-tuple-element.25.refs_0_), channel_id=1, source_target_pairs={{0,1},{1,0},{2,3},{3,2},{4,5},{5,4},{6,7},{7,6},{8,9},{9,8},{10,11... | collective-permute-start | bytes 221192 | tf_op jit(solution)/shard_map/ppermute | solution.py:338
  10.0 0.0 collective-permute-done.refs_1_
  10.0 1.6 %collective-permute-start.8 = (bf16[144,256]{1,0:T(8,128)(2,1)S(1)}, bf16[144,256]{1,0:T(8,128)(2,1)S(1)}, u32[]{:S(2)}, u32[]{:S(2)}) collective-permute-start(bf16[144,256]{1,0:T(8,128)(2,1)S(1)} %get-tuple-element.25.refs_0_), channel_id=1, source_target_pairs={{0,2},{1,3},{2,0},{3,1},{4,6},{5,7},{6,4},{7,5},{8,10},{9,11},{10,... | collective-permute-start | bytes 221192 | tf_op jit(solution)/shard_map/ppermute | solution.py:338
  11.6 0.0 collective-permute-done.1.refs_2_
  11.6 0.4 %collective-permute-start.9 = (bf16[144,256]{1,0:T(8,128)(2,1)S(1)}, bf16[144,256]{1,0:T(8,128)(2,1)S(1)}, u32[]{:S(2)}, u32[]{:S(2)}) collective-permute-start(bf16[144,256]{1,0:T(8,128)(2,1)S(1)} %get-tuple-element.25.refs_0_), channel_id=1, source_target_pairs={{0,3},{1,2},{2,1},{3,0},{4,7},{5,6},{6,5},{7,4},{8,11},{9,10},{10,... | collective-permute-start | bytes 221192 | tf_op jit(solution)/shard_map/ppermute | solution.py:338
  12.0 0.7 %collective-permute-done.10.refs_4_ = bf16[144,256]{1,0:T(8,128)(2,1)S(1)} collective-permute-done((bf16[144,256]{1,0:T(8,128)(2,1)S(1)}, bf16[144,256]{1,0:T(8,128)(2,1)S(1)}, u32[]{:S(2)}, u32[]{:S(2)}) %collective-permute-start.10) | collective-permute-done | bytes 73760 | tf_op jit(solution)/shard_map/ppermute | solution.py:32
  12.8 1.4 %collective-permute-start.11 = (bf16[144,256]{1,0:T(8,128)(2,1)S(1)}, bf16[144,256]{1,0:T(8,128)(2,1)S(1)}, u32[]{:S(2)}, u32[]{:S(2)}) collective-permute-start(bf16[144,256]{1,0:T(8,128)(2,1)S(1)} %collective-permute-done.10.refs_4_), channel_id=1, source_target_pairs={{0,1},{1,0},{2,3},{3,2},{4,5},{5,4},{6,7},{7,6},{8,9},{9,8},{10,11... | collective-permute-start | bytes 221192 | tf_op jit(solution)/shard_map/ppermute | solution.py:338
  14.2 0.0 collective-permute-done.2.refs_3_
  14.2 0.6 %forward.1 = (f32[256,256]{1,0:T(8,128)S(1)}, bf16[256,256]{1,0:T(8,128)(2,1)S(1)}, bf16[256,256]{1,0:T(8,128)(2,1)S(1)}, bf16[256,256]{1,0:T(8,128)(2,1)S(1)}, f32[128,128]{1,0:T(8,128)S(1)}) custom-call(bf16[144,256]{1,0:T(8,128)(2,1)S(1)} %get-tuple-element.17.refs_0_, bf16[144,256]{1,0:T(8,128)(2,1)S(1)} %collective-permute-done.refs_1_, ...), custom_call_target="tpu_custom_call" | custom-call | tf_op jit(solution)/shard_map/forward/pallas_call | solution.py:350
  14.8 0.7 %collective-permute-start.3 = (bf16[256,256]{1,0:T(8,128)(2,1)S(1)}, bf16[256,256]{1,0:T(8,128)(2,1)S(1)}, u32[]{:S(2)}, u32[]{:S(2)}) collective-permute-start(bf16[256,256]{1,0:T(8,128)(2,1)S(1)} %get-tuple-element.20), channel_id=1, source_target_pairs={{0,1},{1,0},{2,3},{3,2},{4,5},{5,4},{6,7},{7,6},{8,9},{9,8},{10,11... | collective-permute-start | bytes 393224 | tf_op jit(solution)/shard_map/ppermute | solution.py:338
  15.5 0.0 collective-permute-done.7.refs_1_
  15.5 1.3 %collective-permute-start.4 = (bf16[256,256]{1,0:T(8,128)(2,1)S(1)}, bf16[256,256]{1,0:T(8,128)(2,1)S(1)}, u32[]{:S(2)}, u32[]{:S(2)}) collective-permute-start(bf16[256,256]{1,0:T(8,128)(2,1)S(1)} %get-tuple-element.21), channel_id=1, source_target_pairs={{0,2},{1,3},{2,0},{3,1},{4,6},{5,7},{6,4},{7,5},{8,10},{9,11},{10,... | collective-permute-start | bytes 393224 | tf_op jit(solution)/shard_map/ppermute | solution.py:338
  16.8 0.0 collective-permute-done.8.refs_2_
  16.8 1.6 %collective-permute-start.5 = (bf16[256,256]{1,0:T(8,128)(2,1)S(1)}, bf16[256,256]{1,0:T(8,128)(2,1)S(1)}, u32[]{:S(2)}, u32[]{:S(2)}) collective-permute-start(bf16[256,256]{1,0:T(8,128)(2,1)S(1)} %get-tuple-element.22), channel_id=1, source_target_pairs={{0,3},{1,2},{2,1},{3,0},{4,7},{5,6},{6,5},{7,4},{8,11},{9,10},{10,... | collective-permute-start | bytes 393224 | tf_op jit(solution)/shard_map/ppermute | solution.py:338
  18.4 0.0 collective-permute-done.9.refs_3_
  18.4 0.9 %collective-permute-start.12 = (bf16[144,256]{1,0:T(8,128)(2,1)S(1)}, bf16[144,256]{1,0:T(8,128)(2,1)S(1)}, u32[]{:S(2)}, u32[]{:S(2)}) collective-permute-start(bf16[144,256]{1,0:T(8,128)(2,1)S(1)} %collective-permute-done.10.refs_4_), channel_id=1, source_target_pairs={{0,2},{1,3},{2,0},{3,1},{4,6},{5,7},{6,4},{7,5},{8,10},{9,11},{10,... | collective-permute-start | bytes 221192 | tf_op jit(solution)/shard_map/ppermute | solution.py:338
  19.3 0.0 collective-permute-done.11.refs_5_
  19.3 1.1 %collective-permute-start.13 = (bf16[144,256]{1,0:T(8,128)(2,1)S(1)}, bf16[144,256]{1,0:T(8,128)(2,1)S(1)}, u32[]{:S(2)}, u32[]{:S(2)}) collective-permute-start(bf16[144,256]{1,0:T(8,128)(2,1)S(1)} %collective-permute-done.10.refs_4_), channel_id=1, source_target_pairs={{0,3},{1,2},{2,1},{3,0},{4,7},{5,6},{6,5},{7,4},{8,11},{9,10},{10,... | collective-permute-start | bytes 221192 | tf_op jit(solution)/shard_map/ppermute | solution.py:338
  20.4 5.2 %collective-permute-done.12.refs_6_ = bf16[144,256]{1,0:T(8,128)(2,1)S(1)} collective-permute-done((bf16[144,256]{1,0:T(8,128)(2,1)S(1)}, bf16[144,256]{1,0:T(8,128)(2,1)S(1)}, u32[]{:S(2)}, u32[]{:S(2)}) %collective-permute-start.12) | collective-permute-done | bytes 73760 | tf_op jit(solution)/shard_map/ppermute | solution.py:338
  25.7 1.6 %collective-permute-done.13.refs_7_ = bf16[144,256]{1,0:T(8,128)(2,1)S(1)} collective-permute-done((bf16[144,256]{1,0:T(8,128)(2,1)S(1)}, bf16[144,256]{1,0:T(8,128)(2,1)S(1)}, u32[]{:S(2)}, u32[]{:S(2)}) %collective-permute-start.13) | collective-permute-done | bytes 73760 | tf_op jit(solution)/shard_map/ppermute | solution.py:338
  27.3 0.7 %backward.1 = (f32[128,256]{1,0:T(8,128)S(1)}, bf16[128,256]{1,0:T(8,128)(2,1)S(1)}, bf16[128,256]{1,0:T(8,128)(2,1)S(1)}, bf16[128,256]{1,0:T(8,128)(2,1)S(1)}, f32[128,128]{1,0:T(8,128)S(1)}) custom-call(bf16[144,256]{1,0:T(8,128)(2,1)S(1)} %get-tuple-element.25.refs_0_, bf16[144,256]{1,0:T(8,128)(2,1)S(1)} %collective-permute-done.7.refs_1_, ...), custom_call_target="tpu_custom_call" | custom-call | tf_op jit(solution)/shard_map/backward/pallas_call | solution.py:376
  28.0 0.1 collective-permute-start.14
  28.0 0.6 %collective-permute-start.15 = (bf16[128,256]{1,0:T(8,128)(2,1)S(1)}, bf16[128,256]{1,0:T(8,128)(2,1)S(1)}, u32[]{:S(2)}, u32[]{:S(2)}) collective-permute-start(bf16[128,256]{1,0:T(8,128)(2,1)S(1)} %get-tuple-element.29), channel_id=1, source_target_pairs={{0,16},{8,24},{16,0},{24,8},{1,17},{9,25},{17,1},{25,9},{2,18},{10... | collective-permute-start | bytes 196616 | tf_op jit(solution)/shard_map/ppermute | solution.py:32
  28.7 0.0 collective-permute-done.3.refs_1_
  28.7 1.2 %collective-permute-start.16 = (bf16[128,256]{1,0:T(8,128)(2,1)S(1)}, bf16[128,256]{1,0:T(8,128)(2,1)S(1)}, u32[]{:S(2)}, u32[]{:S(2)}) collective-permute-start(bf16[128,256]{1,0:T(8,128)(2,1)S(1)} %get-tuple-element.30), channel_id=1, source_target_pairs={{0,24},{8,16},{16,8},{24,0},{1,25},{9,17},{17,9},{25,1},{2,26},{10... | collective-permute-start | bytes 196616 | tf_op jit(solution)/shard_map/ppermute | solution.py:32
  29.9 0.0 collective-permute-done.4.refs_2_
  29.9 0.0 collective-permute-done.5.refs_3_
  29.9 0.1 merge.1
  30.0 2.4 %collective-permute-start.6 = (bf16[128,256]{1,0:T(8,128)(2,1)S(1)}, bf16[128,256]{1,0:T(8,128)(2,1)S(1)}, u32[]{:S(2)}, u32[]{:S(2)}) collective-permute-start(bf16[128,256]{1,0:T(8,128)(2,1)S(1)} %get-tuple-element.24), channel_id=1, source_target_pairs={{0,4},{1,5},{2,6},{3,7},{4,0},{5,1},{6,2},{7,3},{8,12},{9,13},{10,... | collective-permute-start | bytes 196616 | tf_op jit(solution)/shard_map/ppermute | solution.py:32
  32.4 0.0 collective-permute-done.14.refs_1_
  32.4 0.7 %collective-permute-done.15.refs_2_ = bf16[128,256]{1,0:T(8,128)(2,1)S(1)} collective-permute-done((bf16[128,256]{1,0:T(8,128)(2,1)S(1)}, bf16[128,256]{1,0:T(8,128)(2,1)S(1)}, u32[]{:S(2)}, u32[]{:S(2)}) %collective-permute-start.15) | collective-permute-done | bytes 65568 | tf_op jit(solution)/shard_map/ppermute | solution.py:32
  33.1 0.3 collective-permute-done.16.refs_3_
  33.4 0.7 %finish.3 = bf16[128,256]{1,0:T(8,128)(2,1)} custom-call(f32[128,256]{1,0:T(8,128)S(1)} %get-tuple-element.27.refs_0_, bf16[128,256]{1,0:T(8,128)(2,1)S(1)} %collective-permute-done.14.refs_1_, bf16[128,256]{1,0:T(8,128)(2,1)S(1)} %collective-permute-done.15.refs_2_, bf16[128,256]{1,0:T(8,128)(2,1)S(1)} %collective-permute-done.16.refs_3_, ...), custom_call_target="tpu_custom_call" | custom-call | tf_op jit(solution)/shard_map/finish/pallas_call | solution.py:399
  34.1 2.6 %collective-permute-done.6.refs_1_ = bf16[128,256]{1,0:T(8,128)(2,1)S(1)} collective-permute-done((bf16[128,256]{1,0:T(8,128)(2,1)S(1)}, bf16[128,256]{1,0:T(8,128)(2,1)S(1)}, u32[]{:S(2)}, u32[]{:S(2)}) %collective-permute-start.6) | collective-permute-done | bytes 65568 | tf_op jit(solution)/shard_map/ppermute | solution.py:32
  36.7 0.7 %finish.2 = bf16[128,256]{1,0:T(8,128)(2,1)} custom-call(f32[128,256]{1,0:T(8,128)S(1)} %get-tuple-element.23.refs_0_, bf16[128,256]{1,0:T(8,128)(2,1)S(1)} %collective-permute-done.6.refs_1_, f32[128,128]{1,0:T(8,128)S(1)} %get-tuple-element.26.refs_2_), custom_call_target="tpu_custom_call" | custom-call | tf_op jit(solution)/shard_map/finish/pallas_call | solution.py:399
Async XLA Ops:
  2.8 7.2 %collective-permute-start = (bf16[144,256]{1,0:T(8,128)(2,1)S(1)}, bf16[144,256]{1,0:T(8,128)(2,1)S(1)}, u32[]{:S(2)}, u32[]{:S(2)}) collective-permute-start(bf16[144,256]{1,0:T(8,128)(2,1)S(1)} %get-tuple-element.17.refs_0_), channel_id=1, source_target_pairs={{0,8},{8,0},{16,24},{24,16},{1,9},{9,1},{17,25},{25,17},{2,10},{10... | collective-permute-start | bytes 221192 | tf_op jit(solution)/shard_map/ppermute | solution.py:32
  3.4 8.3 %collective-permute-start.1 = (bf16[144,256]{1,0:T(8,128)(2,1)S(1)}, bf16[144,256]{1,0:T(8,128)(2,1)S(1)}, u32[]{:S(2)}, u32[]{:S(2)}) collective-permute-start(bf16[144,256]{1,0:T(8,128)(2,1)S(1)} %get-tuple-element.17.refs_0_), channel_id=1, source_target_pairs={{0,16},{8,24},{16,0},{24,8},{1,17},{9,25},{17,1},{25,9},{2,18},{10... | collective-permute-start | bytes 221192 | tf_op jit(solution)/shard_map/ppermute | solution.py:32
  5.9 6.8 %collective-permute-start.10 = (bf16[144,256]{1,0:T(8,128)(2,1)S(1)}, bf16[144,256]{1,0:T(8,128)(2,1)S(1)}, u32[]{:S(2)}, u32[]{:S(2)}) collective-permute-start(bf16[144,256]{1,0:T(8,128)(2,1)S(1)} %get-tuple-element.25.refs_0_), channel_id=1, source_target_pairs={{0,4},{1,5},{2,6},{3,7},{4,0},{5,1},{6,2},{7,3},{8,12},{9,13},{10,... | collective-permute-start | bytes 221192 | tf_op jit(solution)/shard_map/ppermute | solution.py:32
  8.5 5.7 %collective-permute-start.2 = (bf16[144,256]{1,0:T(8,128)(2,1)S(1)}, bf16[144,256]{1,0:T(8,128)(2,1)S(1)}, u32[]{:S(2)}, u32[]{:S(2)}) collective-permute-start(bf16[144,256]{1,0:T(8,128)(2,1)S(1)} %get-tuple-element.17.refs_0_), channel_id=1, source_target_pairs={{0,24},{8,16},{16,8},{24,0},{1,25},{9,17},{17,9},{25,1},{2,26},{10... | collective-permute-start | bytes 221192 | tf_op jit(solution)/shard_map/ppermute | solution.py:32
  8.5 7.0 %collective-permute-start.7 = (bf16[144,256]{1,0:T(8,128)(2,1)S(1)}, bf16[144,256]{1,0:T(8,128)(2,1)S(1)}, u32[]{:S(2)}, u32[]{:S(2)}) collective-permute-start(bf16[144,256]{1,0:T(8,128)(2,1)S(1)} %get-tuple-element.25.refs_0_), channel_id=1, source_target_pairs={{0,1},{1,0},{2,3},{3,2},{4,5},{5,4},{6,7},{7,6},{8,9},{9,8},{10,11... | collective-permute-start | bytes 221192 | tf_op jit(solution)/shard_map/ppermute | solution.py:338
  10.0 6.8 %collective-permute-start.8 = (bf16[144,256]{1,0:T(8,128)(2,1)S(1)}, bf16[144,256]{1,0:T(8,128)(2,1)S(1)}, u32[]{:S(2)}, u32[]{:S(2)}) collective-permute-start(bf16[144,256]{1,0:T(8,128)(2,1)S(1)} %get-tuple-element.25.refs_0_), channel_id=1, source_target_pairs={{0,2},{1,3},{2,0},{3,1},{4,6},{5,7},{6,4},{7,5},{8,10},{9,11},{10,... | collective-permute-start | bytes 221192 | tf_op jit(solution)/shard_map/ppermute | solution.py:338
  11.6 6.8 %collective-permute-start.9 = (bf16[144,256]{1,0:T(8,128)(2,1)S(1)}, bf16[144,256]{1,0:T(8,128)(2,1)S(1)}, u32[]{:S(2)}, u32[]{:S(2)}) collective-permute-start(bf16[144,256]{1,0:T(8,128)(2,1)S(1)} %get-tuple-element.25.refs_0_), channel_id=1, source_target_pairs={{0,3},{1,2},{2,1},{3,0},{4,7},{5,6},{6,5},{7,4},{8,11},{9,10},{10,... | collective-permute-start | bytes 221192 | tf_op jit(solution)/shard_map/ppermute | solution.py:338
  12.8 6.5 %collective-permute-start.11 = (bf16[144,256]{1,0:T(8,128)(2,1)S(1)}, bf16[144,256]{1,0:T(8,128)(2,1)S(1)}, u32[]{:S(2)}, u32[]{:S(2)}) collective-permute-start(bf16[144,256]{1,0:T(8,128)(2,1)S(1)} %collective-permute-done.10.refs_4_), channel_id=1, source_target_pairs={{0,1},{1,0},{2,3},{3,2},{4,5},{5,4},{6,7},{7,6},{8,9},{9,8},{10,11... | collective-permute-start | bytes 221192 | tf_op jit(solution)/shard_map/ppermute | solution.py:338
  14.8 13.9 %collective-permute-start.3 = (bf16[256,256]{1,0:T(8,128)(2,1)S(1)}, bf16[256,256]{1,0:T(8,128)(2,1)S(1)}, u32[]{:S(2)}, u32[]{:S(2)}) collective-permute-start(bf16[256,256]{1,0:T(8,128)(2,1)S(1)} %get-tuple-element.20), channel_id=1, source_target_pairs={{0,1},{1,0},{2,3},{3,2},{4,5},{5,4},{6,7},{7,6},{8,9},{9,8},{10,11... | collective-permute-start | bytes 393224 | tf_op jit(solution)/shard_map/ppermute | solution.py:338
  15.5 14.4 %collective-permute-start.4 = (bf16[256,256]{1,0:T(8,128)(2,1)S(1)}, bf16[256,256]{1,0:T(8,128)(2,1)S(1)}, u32[]{:S(2)}, u32[]{:S(2)}) collective-permute-start(bf16[256,256]{1,0:T(8,128)(2,1)S(1)} %get-tuple-element.21), channel_id=1, source_target_pairs={{0,2},{1,3},{2,0},{3,1},{4,6},{5,7},{6,4},{7,5},{8,10},{9,11},{10,... | collective-permute-start | bytes 393224 | tf_op jit(solution)/shard_map/ppermute | solution.py:338
  16.8 13.1 %collective-permute-start.5 = (bf16[256,256]{1,0:T(8,128)(2,1)S(1)}, bf16[256,256]{1,0:T(8,128)(2,1)S(1)}, u32[]{:S(2)}, u32[]{:S(2)}) collective-permute-start(bf16[256,256]{1,0:T(8,128)(2,1)S(1)} %get-tuple-element.22), channel_id=1, source_target_pairs={{0,3},{1,2},{2,1},{3,0},{4,7},{5,6},{6,5},{7,4},{8,11},{9,10},{10,... | collective-permute-start | bytes 393224 | tf_op jit(solution)/shard_map/ppermute | solution.py:338
  18.4 7.3 %collective-permute-start.12 = (bf16[144,256]{1,0:T(8,128)(2,1)S(1)}, bf16[144,256]{1,0:T(8,128)(2,1)S(1)}, u32[]{:S(2)}, u32[]{:S(2)}) collective-permute-start(bf16[144,256]{1,0:T(8,128)(2,1)S(1)} %collective-permute-done.10.refs_4_), channel_id=1, source_target_pairs={{0,2},{1,3},{2,0},{3,1},{4,6},{5,7},{6,4},{7,5},{8,10},{9,11},{10,... | collective-permute-start | bytes 221192 | tf_op jit(solution)/shard_map/ppermute | solution.py:338
  19.3 8.0 %collective-permute-start.13 = (bf16[144,256]{1,0:T(8,128)(2,1)S(1)}, bf16[144,256]{1,0:T(8,128)(2,1)S(1)}, u32[]{:S(2)}, u32[]{:S(2)}) collective-permute-start(bf16[144,256]{1,0:T(8,128)(2,1)S(1)} %collective-permute-done.10.refs_4_), channel_id=1, source_target_pairs={{0,3},{1,2},{2,1},{3,0},{4,7},{5,6},{6,5},{7,4},{8,11},{9,10},{10,... | collective-permute-start | bytes 221192 | tf_op jit(solution)/shard_map/ppermute | solution.py:338
  28.0 4.4 %collective-permute-start.14 = (bf16[128,256]{1,0:T(8,128)(2,1)S(1)}, bf16[128,256]{1,0:T(8,128)(2,1)S(1)}, u32[]{:S(2)}, u32[]{:S(2)}) collective-permute-start(bf16[128,256]{1,0:T(8,128)(2,1)S(1)} %get-tuple-element.28), channel_id=1, source_target_pairs={{0,8},{8,0},{16,24},{24,16},{1,9},{9,1},{17,25},{25,17},{2,10},{10... | collective-permute-start | bytes 196616 | tf_op jit(solution)/shard_map/ppermute | solution.py:32
  28.0 5.0 %collective-permute-start.15 = (bf16[128,256]{1,0:T(8,128)(2,1)S(1)}, bf16[128,256]{1,0:T(8,128)(2,1)S(1)}, u32[]{:S(2)}, u32[]{:S(2)}) collective-permute-start(bf16[128,256]{1,0:T(8,128)(2,1)S(1)} %get-tuple-element.29), channel_id=1, source_target_pairs={{0,16},{8,24},{16,0},{24,8},{1,17},{9,25},{17,1},{25,9},{2,18},{10... | collective-permute-start | bytes 196616 | tf_op jit(solution)/shard_map/ppermute | solution.py:32
  28.7 4.7 %collective-permute-start.16 = (bf16[128,256]{1,0:T(8,128)(2,1)S(1)}, bf16[128,256]{1,0:T(8,128)(2,1)S(1)}, u32[]{:S(2)}, u32[]{:S(2)}) collective-permute-start(bf16[128,256]{1,0:T(8,128)(2,1)S(1)} %get-tuple-element.30), channel_id=1, source_target_pairs={{0,24},{8,16},{16,8},{24,0},{1,25},{9,17},{17,9},{25,1},{2,26},{10... | collective-permute-start | bytes 196616 | tf_op jit(solution)/shard_map/ppermute | solution.py:32
  30.0 6.7 %collective-permute-start.6 = (bf16[128,256]{1,0:T(8,128)(2,1)S(1)}, bf16[128,256]{1,0:T(8,128)(2,1)S(1)}, u32[]{:S(2)}, u32[]{:S(2)}) collective-permute-start(bf16[128,256]{1,0:T(8,128)(2,1)S(1)} %get-tuple-element.24), channel_id=1, source_target_pairs={{0,4},{1,5},{2,6},{3,7},{4,0},{5,1},{6,2},{7,3},{8,12},{9,13},{10,... | collective-permute-start | bytes 196616 | tf_op jit(solution)/shard_map/ppermute | solution.py:32
